TPU v7x, 256 devices: a whole 4x4x8 slice. The times are simulated.
256 devices in a mesh: ta: 64 (over y, z, x_hi), gz: 4 (over x_lo, core).
Axes of the slice: x: 4 (x_hi: 2, x_lo: 2; x = x_hi * 2 + x_lo), y: 4, z: 8, core: 2. Of those that a mesh axis runs over, the one named last changes fastest.
Arguments:
- eigvecs: bfloat16 [64, 2, 3, 16, 256, 128], P('ta', None, None, 'gz'), may hold values from -6 to 6
- gauge_links: bfloat16 [64, 3, 3, 3, 2, 16, 256], P('ta', None, None, None, None, 'gz'), may hold values from -2.5 to 2.5
- peramb: bfloat16 [64, 4, 4, 4, 2, 128, 128], P('ta', None, 'gz'), may hold values from -0.3984375 to 0.3984375
- momenta: int32 [2, 3], replicated, may hold values from -2 to 2
- disp_paths: int32 [2, 2], replicated, may hold values from 1 to 3, as said below
- sources: int32 [4], replicated, may hold values from 0 to 63
Outputs:
- elementals: bfloat16 [64, 2, 2, 2, 128, 128], P('ta', None, None, None, 'gz')
- correlator: float32 [4, 64, 2, 2, 2], P(None, 'ta')
Inputs may be any that keep to these rules, and one draw needn't show every extreme that they name: `disp_paths`: in each momentum's row exactly one path runs along the third dimension (value 3); every other path is 1 or 2.
All inputs are finite; a program needn't handle non-finite values.
Results may differ from a plain program's by a relative error of at most 0.0081.
Values may be sent and summed in bfloat16 or wider, within the bound.
No kernel may reach another device: no remote copies, remote signals or barrier semaphores. Data moves between devices by JAX's collectives and lax.ppermute only.
A program may use at most 128 MiB of HBM per device.

v0:
```python
import math

import jax
import jax.numpy as jnp
from jax import lax
from jax.sharding import PartitionSpec as P

LX = 16
LY = 16
NSRC = 4


HIGHEST = lax.Precision.HIGHEST


def from_behind(block, axis, distance):
    devices = range(lax.axis_size(axis))
    route = [((i - distance) % len(devices), i) for i in devices]
    return lax.ppermute(block, axis, route)


def from_root(value, axis, source):
    kept = jnp.where(lax.axis_index(axis) == source, value, 0).astype(value.dtype)
    return lax.psum(kept, axis)


def transport(link_dir, source):
    link_re = link_dir[:, :, 0].astype(jnp.float32)
    link_im = link_dir[:, :, 1].astype(jnp.float32)
    source_re = source[0].astype(jnp.float32)
    source_im = source[1].astype(jnp.float32)
    total_re = jnp.zeros(source_re.shape, jnp.float32)
    total_im = jnp.zeros(source_re.shape, jnp.float32)
    for colour in range(3):
        coef_re = link_re[:, colour][..., None]
        coef_im = link_im[:, colour][..., None]
        total_re = total_re + coef_re * source_re[colour][None] - coef_im * source_im[colour][None]
        total_im = total_im + coef_re * source_im[colour][None] + coef_im * source_re[colour][None]
    return jnp.stack([total_re, total_im])


def back_transport(link_dir, source):
    link_re = link_dir[:, :, 0].astype(jnp.float32)
    link_im = link_dir[:, :, 1].astype(jnp.float32)
    source_re = source[0].astype(jnp.float32)
    source_im = source[1].astype(jnp.float32)
    total_re = jnp.zeros(source_re.shape, jnp.float32)
    total_im = jnp.zeros(source_re.shape, jnp.float32)
    for colour in range(3):
        coef_re = link_re[colour][..., None]
        coef_im = link_im[colour][..., None]
        total_re = total_re + coef_re * source_re[colour][None] + coef_im * source_im[colour][None]
        total_im = total_im + coef_re * source_im[colour][None] - coef_im * source_re[colour][None]
    return jnp.stack([total_re, total_im])


def phase_table(momentum, zcoord, lz_total):
    xcoord = jnp.arange(LX, dtype=jnp.int32)
    ycoord = jnp.arange(LY, dtype=jnp.int32)
    volume = LX * LY * lz_total
    phase_int = (
        momentum[0] * xcoord[None, :, None] * (LY * lz_total)
        + momentum[1] * ycoord[None, None, :] * (LX * lz_total)
        + momentum[2] * zcoord[:, None, None] * (LX * LY)
    )
    phase_int = jnp.mod(phase_int, volume)
    angles = phase_int.astype(jnp.float32) * (2.0 * math.pi / volume)
    return (jnp.cos(angles), jnp.sin(angles))


def elementals_one(vectors, selected, momentum, zcoord, lz_total):
    cosine, sine_table = phase_table(momentum, zcoord, lz_total)
    cosine = cosine[None, :, :, :, None]
    sine_table = sine_table[None, :, :, :, None]
    vec_re = vectors[0].astype(jnp.float32)
    vec_im = vectors[1].astype(jnp.float32)
    phased = jnp.stack(
        [vec_re * cosine - vec_im * sine_table, -(vec_re * sine_table + vec_im * cosine)]
    ).astype(jnp.bfloat16)
    num_vec = vectors.shape[-1]
    phased_rows = phased.reshape(2, -1, num_vec)
    displaced_cols = selected.reshape(selected.shape[0], 2, -1, num_vec)
    products = lax.dot_general(
        phased_rows, displaced_cols, (((1,), (2,)), ((), ())), preferred_element_type=jnp.float32
    )
    real_part = products[0, :, :, 0] - products[1, :, :, 1]
    imag_part = products[0, :, :, 1] + products[1, :, :, 0]
    return jnp.transpose(jnp.stack([real_part, imag_part]), (2, 0, 1, 3))


def block_real(values, part_axis):
    real_half = jnp.take(values, 0, axis=part_axis)
    imag_half = jnp.take(values, 1, axis=part_axis)
    first_row = jnp.stack([real_half, imag_half], axis=part_axis)
    second_row = jnp.stack([-imag_half, real_half], axis=part_axis)
    return jnp.stack([first_row, second_row], axis=part_axis)


def contraction(sink_phi, source_phi, peramb_slice):
    peramb_block = block_real(peramb_slice, 3)
    sink_side = lax.dot_general(
        sink_phi, peramb_block, (((2, 4), (3, 5)), ((), ())), preferred_element_type=jnp.float32
    )
    source_block = block_real(source_phi, 3)
    image_side = lax.dot_general(
        peramb_slice,
        source_block,
        (((3, 5), (3, 5)), ((0,), (0,))),
        preferred_element_type=jnp.float32,
    )
    table = lax.dot_general(
        sink_side,
        image_side,
        (((4, 5, 2, 7), (1, 2, 3, 7)), ((3, 0, 1), (0, 4, 5))),
        precision=HIGHEST,
        preferred_element_type=jnp.float32,
    )
    real_sum = table[..., 0, 0] + table[..., 1, 1]
    imag_sum = table[..., 1, 0] - table[..., 0, 1]
    return jnp.stack([real_sum, imag_sum], axis=-1)


def on_device(eigvecs, gauge_links, peramb, momenta, disp_paths, sources):
    num_vec = eigvecs.shape[-1]
    z_depth = eigvecs.shape[3]
    groups = lax.axis_size("gz")
    lz_total = z_depth * groups
    row_count = num_vec // groups
    vectors = eigvecs[0].reshape(2, 3, z_depth, LX, LY, num_vec)
    links_slice = gauge_links[0].reshape(3, 3, 3, 2, z_depth, LX, LY)
    results = []
    for direction in range(2):
        axis_id = (3, 4)[direction]
        link_dir = links_slice[direction]
        shifted_up = jnp.roll(vectors, -1, axis=axis_id)
        forward = transport(link_dir, shifted_up)
        backward = back_transport(link_dir, vectors).astype(jnp.bfloat16)
        behind = jnp.roll(backward, 1, axis=axis_id).astype(jnp.float32)
        results.append((forward - behind).astype(jnp.bfloat16))
    link_dir = links_slice[2]
    top_plane = from_behind(vectors[:, :, :1], "gz", -1)
    shifted_up = jnp.concatenate([vectors[:, :, 1:], top_plane], axis=2)
    forward = transport(link_dir, shifted_up)
    backward = back_transport(link_dir, vectors).astype(jnp.bfloat16)
    bottom_plane = from_behind(backward[:, :, -1:], "gz", 1)
    behind = jnp.concatenate([bottom_plane, backward[:, :, :-1]], axis=2).astype(jnp.float32)
    results.append((forward - behind).astype(jnp.bfloat16))
    displaced = jnp.stack(results)
    zcoord = lax.axis_index("gz") * z_depth + jnp.arange(z_depth, dtype=jnp.int32)

    def one_momentum(pair):
        selected = jnp.take(displaced, pair[1] - 1, axis=0)
        return elementals_one(vectors, selected, pair[0], zcoord, lz_total)

    partial_value = lax.map(one_momentum, (momenta, disp_paths))
    norm_scale = 1.0 / math.sqrt(12.0 * LX * LY * lz_total)
    full_sum = lax.psum(partial_value, "gz")
    sink_phi = (full_sum * norm_scale).astype(jnp.bfloat16)
    rows_phi = lax.dynamic_slice_in_dim(sink_phi, lax.axis_index("gz") * row_count, row_count, 3)
    received = []
    for source_slot in range(NSRC):
        received.append(from_root(sink_phi, "ta", sources[source_slot]))
    source_phi = jnp.stack(received)
    corr_terms = contraction(sink_phi, source_phi, peramb[0])
    summed = lax.psum(corr_terms, "gz") / (8.0 * num_vec)
    return (rows_phi[None], summed[:, None])


def solution(mesh):
    placed = (
        P("ta", None, None, "gz", None, None),
        P("ta", None, None, None, None, "gz", None),
        P("ta", None, "gz", None, None, None, None),
        P(),
        P(),
        P(),
    )
    return jax.shard_map(
        on_device,
        mesh=mesh,
        in_specs=placed,
        out_specs=(P("ta", None, None, None, "gz", None), P(None, "ta", None, None, None)),
        check_vma=False,
    )
```

profile of v0, /device:TPU:1, one launch (start us, length us, event | category | flops | bytes accessed | tf_op | source)
XLA Modules:
  0.0 958.8 jit_solution(7554409827072167682)
XLA Ops:
  7.2 1.8 slice.725
  9.0 3.2 collective-permute-start
  12.2 1.7 slice_convert_fusion.1
  15.6 3.4 add_convert_fusion
  20.1 1.0 copy_convert_fusion.4
  23.3 6.0 add_convert_fusion.2
  29.5 1.2 copy-done
  31.9 1.1 fusion.39
  35.3 1.5 fusion.37
  37.8 2.5 subtract_bitcast_fusion.2
  40.9 5.3 subtract_bitcast_fusion.1
  47.1 1.2 slice.724
  50.1 3.3 fusion.32
  53.5 1.2 fusion.45
  55.7 2.5 subtract_bitcast_fusion
  58.2 1.5 fusion.33
  60.3 3.4 copy.143
  63.7 24.4 %while.19 = (s32[]{:T(128)}, f32[2,2,2,128,128]{4,3,2,1,0:T(8,128)}, bf16[2,3,4,16,16,128]{5,4,3,2,1,0:T(8,128)(2,1)S(1)}, s32[2,3]{1,0:T(2,128)S(1)}, s32[2,2]{...) while((s32[]{:T(128)}, ...), condition=%wide.region_1.2_spmd.clone, body=%wide.region_0.1_spmd.clone.sunk | while | flops 814497152 | bytes 16014317 | solution.py:155
  64.4 1.2 multiply_multiply_fusion.3
  67.2 5.0 gather_fusion
  72.2 3.0 fusion.135
  76.6 1.2 multiply_multiply_fusion.3
  79.4 5.0 gather_fusion
  84.4 3.0 fusion.135
  91.6 41.8 %all-reduce.4.cloned.1.call-done = f32[2,2,2,128,128]{4,3,2,1,0:T(8,128)} async-done(((f32[2,2,2,128,128]{4,3,2,1,0:T(8,128)}), f32[2,2,2,128,128]{4,3,2,1,0:T(8,128)}) %all-reduce.4.cloned.1.call-update) | async-done | bytes 524304 | tf_op jit(solution)/shard_map/psum | solution.py:157
  133.3 1.9 select_bitcast_fusion
  137.2 4.6 convolution_bitcast_fusion
  141.8 645.3 %all-reduce.6.cloned.1.call-done = (bf16[1,2,2,2,128,128]{5,4,3,2,1,0:T(8,128)(2,1)}, bf16[1,2,2,2,128,128]{5,4,3,2,1,0:T(8,128)(2,1)}, bf16[1,2,2,2,128,128]{5,...) async-done(((bf16[1,2,2,2,128,128]{5,4,3,2,1,0:T(8,128)(2,1)}, bf16[1,2,2,2,128,128]{5,4,3,2,1,0:T(8,128)(2,1)}, bf16[1,2,2,2,128,128]{5,4,3,2,1,0:T(8,128)(2,1)}, ...) | async-done | bytes 1048592 | tf_op jit(solution)/shard_map/psum | solution.py:24
  790.5 4.8 convolution_bitcast_fusion.1
  795.4 13.2 %copy.151 = f32[4,4,128,2,2,2,128]{6,5,2,1,4,3,0:T(2,128)} copy(f32[4,4,128,2,2,2,128]{2,6,1,5,4,3,0:T(8,128)} %convolution_bitcast_fusion.1) | data formatting | bytes 16777216 | tf_op jit(solution)/shard_map/dot_general | solution.py:105
  808.5 90.4 %fusion.40 = f32[4,2,2,2,2]{4,3,2,1,0:T(2,128)S(1)} fusion(f32[4,4,128,2,2,2,128]{6,5,2,1,4,3,0:T(2,128)} %copy.151, f32[2,2,128,4,4,2,128]{6,2,5,4,3,1,0:T(8,128)} %convolution_bitcast_fusion), kind=kOutput, calls=%fused_computation.92 | convolution fusion | flops 50331648 | bytes 16777472 | tf_op jit(solution)/shard_map/dot_general | solution.py:111
  899.2 51.8 %psum.47 = f32[4,2,2,2]{0,2,3,1:T(2,128)S(1)} all-reduce(f32[4,2,2,2]{0,2,3,1:T(2,128)S(1)} %pad_maximum_fusion.9), channel_id=1, replica_groups=mesh['ta'=64,'gz'=4] {'gz'}, use_global_device_ids=true, to_apply=%region_7.12 | all-reduce | flops 32 | bytes 256 | tf_op jit(solution)/shard_map/psum | solution.py:165
  (142 shorter events, 27.0 us)
Async XLA Ops:
  7.2 126.2 %all-reduce.4.cloned.1.call-start = ((), (), s32[]{:S(2)}) async-start(), calls=%async_computation | async-start | bytes 1048576 | tf_op jit(solution)/shard_map/psum | solution.py:157
  9.0 5.0 copy-start.22
  9.0 44.5 %collective-permute-start = (bf16[2,3,1,16,16,128]{5,4,3,2,1,0:T(8,128)(2,1)}, bf16[2,3,1,16,16,128]{5,4,3,2,1,0:T(8,128)(2,1)}, u32[]{:S(2)}, u32[]{:S(2)}) collective-permute-start(bf16[2,3,1,16,16,128]{5,4,3,2,1,0:T(8,128)(2,1)} %slice.725), channel_id=1, source_target_pairs={{1,0},{2,1},{3,2},{0,3},{5,4},{6,5},{7,6},{4,7},{9,8},{10,9},{11,1... | collective-permute-start | bytes 1179656 | tf_op jit(solution)/shard_map/ppermute | solution.py:19
  15.5 3.5 copy-start.1
  15.5 3.5 copy-start.3
  15.5 3.5 copy-start.5
  15.6 3.5 copy-start.7
  15.6 3.5 copy-start.9
  15.6 3.5 copy-start.11
  19.8 38.3 %collective-permute-start.1 = (bf16[2,3,1,16,16,128]{5,4,2,1,0,3:T(8,128)(2,1)}, bf16[2,3,1,16,16,128]{5,4,2,1,0,3:T(8,128)(2,1)}, u32[]{:S(2)}, u32[]{:S(2)}) collective-permute-start(bf16[2,3,1,16,16,128]{5,4,2,1,0,3:T(8,128)(2,1)} %pad_maximum_fusion.7), channel_id=1, source_target_pairs={{3,0},{0,1},{1,2},{2,3},{7,4},{4,5},{5,6},{6,7},{11,8},{8,9},{9,10... | collective-permute-start | bytes 1179656 | tf_op jit(solution)/shard_map/ppermute | solution.py:19
  21.5 1.0 copy-start.2
  21.5 1.2 copy-start.4
  21.5 1.3 copy-start.6
  21.5 1.5 copy-start.8
  21.5 1.6 copy-start.10
  21.5 1.8 copy-start.12
  29.3 1.4 copy-start
  31.8 1.3 copy-start.18
  31.9 1.2 copy-start.17
  33.0 1.0 copy-start.16
  50.1 3.4 copy-start.13
  54.7 0.9 copy-start.19
  54.7 0.9 copy-start.20
  55.7 2.5 copy-start.14
  60.3 3.4 copy-start.24
  60.3 3.4 copy-start.25
  63.7 24.5 %copy-start.23 = (s32[4]{0:T(128)S(1)}, s32[4]{0:T(128)}, u32[]{:S(2)}) copy-start(s32[4]{0:T(128)} %param.21) | copy-start | bytes 52
  88.2 698.9 %all-reduce.6.cloned.1.call-start = ((), (), s32[]{:S(2)}) async-start(), calls=%async_computation.1 | async-start | bytes 2097152 | tf_op jit(solution)/shard_map/psum | solution.py:24
  91.6 44.6 %copy-start.15 = (bf16[1,4,1,4,2,128,128]{6,5,4,3,2,1,0:T(8,128)(2,1)S(1)}, bf16[1,4,1,4,2,128,128]{6,5,4,3,2,1,0:T(8,128)(2,1)}, u32[]{:S(2)}) copy-start(bf16[1,4,1,4,2,128,128]{6,5,4,3,2,1,0:T(8,128)(2,1)} %param.18) | copy-start | bytes 3145732
  787.1 3.0 copy-start.21
Sparse Core Ops, SparseCore 0:
  88.3 44.9 all-reduce.3
  136.3 650.8 all-reduce.5
where the time goes:
time: 968 us; the launch traced here: 959 us
  waiting for transfers between devices  687 us (71%)
  matrix products  106 us (11%)
  blocking collectives  51.8 us (5%)
  other arithmetic  46.6 us (5%)
  local copies, waits for them, and re-layouts  46.4 us (5%)
  between operations  17.8 us (2%)
    psum x1, waiting for transfers between devices, from_root(): return lax.psum(kept, axis)  645 us
    dot_general x1, matrix products, contraction(): lax.dot_general(sink_side, image_side, (((4, 5, 2, 7), (1, 2, 3, 7)), ((3...  90.4 us
    psum x1, blocking collectives, on_device(): summed = lax.psum(corr_terms, 'gz') / (8.0 * num_vec)  51.8 us
    psum x1, waiting for transfers between devices, on_device(): full_sum = lax.psum(partial_value, 'gz')  41.8 us
  transfers between devices with their start and end apart: 4, of which 2 were waited for; matrix products, arithmetic and copies ran while one was open for 5% of the time, Pallas kernels for 0%

commit v1 on v0

v1 whole, which is shorter than its diff:
```python
import functools
import math

import jax
import jax.numpy as jnp
import numpy as np
from jax import lax
from jax.experimental import pallas as pl
from jax.experimental.pallas import tpu as pltpu
from jax.sharding import Mesh
from jax.sharding import PartitionSpec as P

LX = 16
LY = 16
NSRC = 4
BF = jnp.bfloat16
F32 = jnp.float32
NT_DIMS = (((1,), (1,)), ((), ()))
TA = ("y", "z", "xh")
YZ = ("y", "z")
GZ = ("xl", "c")


def dot_nt(a, b):
    return lax.dot_general(a, b, NT_DIMS, preferred_element_type=F32)


def dot_nn(a, b):
    return jnp.dot(a, b, preferred_element_type=F32)


def shift_matrix(direction):
    row = lax.broadcasted_iota(jnp.int32, (256, 256), 0)
    col = lax.broadcasted_iota(jnp.int32, (256, 256), 1)
    if direction == 0:
        target = (col + LY) & 255
    else:
        target = (col & ~(LY - 1)) | ((col + 1) & (LY - 1))
    return jnp.where(row == target, 1.0, 0.0).astype(F32).astype(BF)


def unit_matrix(n):
    row = lax.broadcasted_iota(jnp.int32, (n, n), 0)
    col = lax.broadcasted_iota(jnp.int32, (n, n), 1)
    return jnp.where(row == col, 1.0, 0.0).astype(F32).astype(BF)


def transport(links, z, direction, source, target):
    for half in range(2):
        lanes = pl.ds(half * 128, 128)
        coef = [
            [
                [
                    jnp.broadcast_to(
                        links[z, pl.ds(direction * 18 + a * 6 + b * 2 + part, 1), lanes], (8, 128)
                    )
                    for part in range(2)
                ]
                for b in range(3)
            ]
            for a in range(3)
        ]

        def rows(step, _):
            parts = []
            for sub in range(2):
                at = pl.ds(pl.multiple_of(step * 16 + sub * 8, 8), 8)
                vec = [[source(part * 3 + b, at, lanes) for b in range(3)] for part in range(2)]
                out = []
                for a in range(3):
                    re = im = None
                    for b in range(3):
                        ur, ui = coef[a][b]
                        tr = ur * vec[0][b] - ui * vec[1][b]
                        ti = ur * vec[1][b] + ui * vec[0][b]
                        re = tr if re is None else re + tr
                        im = ti if im is None else im + ti
                    out.append((re, im))
                parts.append(out)
            for a in range(3):
                for part in range(2):
                    block = jnp.concatenate([parts[0][a][part], parts[1][a][part]], axis=0)
                    target[
                        pl.ds(pl.multiple_of(part * 128 + step * 16, 16), 16),
                        pl.ds(a * 256 + half * 128, 128),
                    ] = block.astype(BF)
            return 0

        lax.fori_loop(0, 8, rows, 0, unroll=2)


def phase_rows(ints, row, plane):
    site = lax.broadcasted_iota(jnp.int32, (8, 256), 1)
    x1 = site >> 4
    x2 = site & (LY - 1)
    steps = ints[row * 3] * x1 + ints[row * 3 + 1] * x2 + ints[row * 3 + 2] * plane
    angle = (steps & 15).astype(F32) * (2.0 * math.pi / 16.0)
    return jnp.cos(angle), jnp.sin(angle)


def local_kernel(ints, eig, links, acc, phased, vt, vs, field, perm):
    unit = unit_matrix(128)
    perm[0] = shift_matrix(0)
    perm[1] = shift_matrix(1)

    def load(z, _):
        for comp in range(6):
            vt[z, comp] = dot_nt(unit, eig[comp // 3, comp % 3, z])
        return 0

    lax.fori_loop(0, 4, load, 0)
    acc[...] = jnp.zeros_like(acc)

    def plane(z, _):
        for m in range(2):
            cosine, sine = phase_rows(ints, m, ints[10] + z)

            def rows(step, _):
                at = pl.ds(pl.multiple_of(step * 16, 16), 16)
                for half in range(2):
                    lanes = pl.ds(half * 128, 128)
                    cs = jnp.concatenate([cosine[:, half * 128 : half * 128 + 128]] * 2, axis=0)
                    sn = jnp.concatenate([sine[:, half * 128 : half * 128 + 128]] * 2, axis=0)
                    for a in range(3):
                        re = vt[z, a, at, lanes]
                        im = vt[z, 3 + a, at, lanes]
                        rc, rs, ic, js = re * cs, re * sn, im * cs, im * sn
                        to = pl.ds(a * 256 + half * 128, 128)
                        for block, value in enumerate((rc - js, -(rs + ic), rc + js, rs - ic)):
                            phased[
                                m, pl.ds(pl.multiple_of(block * 128 + step * 16, 16), 16), to
                            ] = value.astype(BF)
                return 0

            lax.fori_loop(0, 8, rows, 0)
        for direction in range(2):
            vs[...] = dot_nn(vt[z].reshape(768, 256).astype(BF), perm[direction]).reshape(
                6, 128, 256
            )
            transport(
                links, z, direction, lambda comp, at, lanes: vs[comp, at, lanes], field.at[direction]
            )
        for m in range(2):
            which = jnp.where(ints[6 + 2 * m] == 3, ints[7 + 2 * m], ints[6 + 2 * m]) - 1
            acc[2 * m + 1] += dot_nt(phased[m], field[which])

        @pl.when(z < 3)
        def _():
            transport(
                links, z, 2, lambda comp, at, lanes: vt[z + 1, comp, at, lanes], field.at[2]
            )
            for m in range(2):
                acc[2 * m] += dot_nt(phased[m], field[2])

        return 0

    lax.fori_loop(0, 4, plane, 0)


def edge_kernel(ints, shifts, halo, links, acc, phased, out, vt, field):
    unit = unit_matrix(128)
    for comp in range(6):
        vt[comp] = dot_nt(unit, halo[comp // 3, comp % 3])
    transport(links, 0, 2, lambda comp, at, lanes: vt[comp, at, lanes], field)
    for m in range(2):
        along = jnp.where(ints[6 + 2 * m] == 3, 0, 1)
        for o in range(2):
            t = acc[2 * m + o]
            if o == 0:
                t = t + dot_nt(phased[m], field[...])
                slot = along
            else:
                slot = 1 - along
            direction = ints[6 + 2 * m + slot] - 1
            cd = shifts[2 * (m * 3 + direction)]
            sd = shifts[2 * (m * 3 + direction) + 1]
            ar = t[0:128, 0:128] - t[128:256, 128:256]
            ai = t[0:128, 128:256] + t[128:256, 0:128]
            br = (t[256:384, 0:128] - t[384:512, 128:256]).T
            bi = (t[256:384, 128:256] + t[384:512, 0:128]).T
            out[2 * m + slot, 0] = ar - cd * br + sd * bi
            out[2 * m + slot, 1] = ai + sd * br + cd * bi


def loop_kernel(phi, tau0, tau1, tau2, tau3, out):
    lhs = jnp.concatenate([phi[0], phi[1]], axis=1)

    def slot(s, _):
        total = jnp.zeros((128, 256), F32)
        for tau in (tau0, tau1, tau2, tau3):
            for beta in range(4):
                tr = tau[s, beta, 0]
                ti = tau[s, beta, 1]
                rhs = jnp.concatenate(
                    [jnp.concatenate([tr, ti], axis=1), jnp.concatenate([-ti, tr], axis=1)], axis=0
                )
                mid = dot_nn(lhs, rhs).astype(BF)
                zr, zi = mid[:, :128], mid[:, 128:]
                rhs = jnp.concatenate(
                    [jnp.concatenate([zr, zi], axis=1), jnp.concatenate([zi, -zr], axis=1)], axis=0
                )
                left = jnp.concatenate([tr, ti], axis=0)
                total = total + lax.dot_general(
                    left, rhs, (((0,), (0,)), ((), ())), preferred_element_type=F32
                )
        out[s, 0] = total[:, :128]
        out[s, 1] = total[:, 128:]
        return 0

    lax.fori_loop(0, 4, slot, 0)


VMEM = pl.BlockSpec(memory_space=pltpu.VMEM)
SMEM = pl.BlockSpec(memory_space=pltpu.SMEM)


def call(kernel, outs, inputs, scratch, flops, moved):
    return pl.pallas_call(
        kernel,
        out_shape=outs,
        in_specs=[SMEM if x.ndim == 1 else VMEM for x in inputs],
        out_specs=jax.tree.map(lambda _: VMEM, outs),
        scratch_shapes=scratch,
        compiler_params=pltpu.CompilerParams(vmem_limit_bytes=48 * 2**20),
        cost_estimate=pl.CostEstimate(flops=flops, bytes_accessed=moved, transcendentals=0),
    )(*inputs)


def partner(value, axis, distance=1):
    n = lax.axis_size(axis)
    return lax.ppermute(value, axis, [((i + distance) % n, i) for i in range(n)])


def on_device(eigvecs, gauge_links, peramb, momenta, disp_paths, sources):
    eig = eigvecs[0]
    depth = eig.shape[2]
    lower = lax.axis_index("xl") * 2 + lax.axis_index("c")
    halo_out = eig[:, :, 0]
    halo = lax.ppermute(halo_out, GZ, [((i + 1) % 4, i) for i in range(4)])
    links = jnp.swapaxes(gauge_links[0].reshape(54, depth, LX * LY), 0, 1).astype(F32)
    ints = jnp.concatenate(
        [momenta.reshape(6), disp_paths.reshape(4), (lower * depth)[None].astype(jnp.int32)]
    )
    turn = (momenta.reshape(6) & 15).astype(F32) * (2.0 * math.pi / 16.0)
    shifts = jnp.stack([jnp.cos(turn), jnp.sin(turn)], axis=1).reshape(12)
    acc, phased = call(
        local_kernel,
        (jax.ShapeDtypeStruct((4, 512, 256), F32), jax.ShapeDtypeStruct((2, 512, 768), BF)),
        (ints, eig, links),
        [
            pltpu.VMEM((4, 6, 128, 256), F32),
            pltpu.VMEM((6, 128, 256), F32),
            pltpu.VMEM((3, 256, 768), BF),
            pltpu.VMEM((2, 256, 256), BF),
        ],
        4 * 10**9,
        5 * 10**6,
    )
    partial = call(
        edge_kernel,
        jax.ShapeDtypeStruct((4, 2, 128, 128), F32),
        (ints, shifts, halo, links[depth - 1 :], acc, phased),
        [pltpu.VMEM((6, 128, 256), F32), pltpu.VMEM((256, 768), BF)],
        5 * 10**8,
        5 * 10**6,
    )
    norm_scale = 1.0 / math.sqrt(12.0 * LX * LY * depth * 4)
    shares = lax.all_to_all(partial, GZ, 0, 0, tiled=True)
    phi = (jnp.sum(shares, axis=0) * norm_scale).astype(BF)

    chunks = lax.all_to_all(phi.reshape(32, 8, 128), YZ, 0, 0, tiled=True)
    mine = (sources & 1) == lax.axis_index("xh")
    picked = jnp.stack(
        [lax.dynamic_index_in_dim(chunks, sources[s] >> 1, 0, keepdims=False) for s in range(NSRC)]
    )
    other = lax.ppermute(picked, "xh", [(0, 1), (1, 0)])
    picked = jnp.where(mine[:, None, None], picked, other)
    spread = jnp.broadcast_to(picked[None], (32, NSRC, 8, 128))
    source_phi = lax.all_to_all(spread, YZ, 0, 0, tiled=True)
    source_phi = jnp.swapaxes(source_phi, 0, 1).reshape(NSRC, 2, 128, 128).astype(F32)

    tau = peramb[0, :, 0]
    tau, phi_held = lax.optimization_barrier((tau, phi))
    tau_far = partner(tau, "xl")
    tau_near = partner(tau, "c")
    tau_diag = partner(tau_far, "c")
    looped = call(
        loop_kernel,
        jax.ShapeDtypeStruct((NSRC, 2, 128, 128), F32),
        (phi_held, tau, tau_near, tau_far, tau_diag),
        [],
        2 * 10**9,
        5 * 10**6,
    )
    real = jnp.sum(looped * source_phi, axis=(1, 2, 3))
    imag = jnp.sum(looped[:, 1] * source_phi[:, 0] - looped[:, 0] * source_phi[:, 1], axis=(1, 2))
    pair = jnp.stack([real, imag], axis=-1) / (8.0 * 128)
    owned = jnp.arange(4, dtype=jnp.int32) == lower
    spreadout = jnp.where(owned[None, :, None], pair[:, None, :], 0.0)
    correlator = lax.psum(spreadout, GZ).reshape(NSRC, 1, 2, 2, 2)

    rows = lax.all_to_all(
        jnp.swapaxes(phi.reshape(2, 4, 32, 128), 0, 1), GZ, 0, 0, tiled=True
    )
    return rows.reshape(1, 2, 2, 2, 32, 128), correlator


def solution(mesh):
    fine = Mesh(np.asarray(mesh.devices).reshape(4, 8, 2, 2, 2), (*TA, *GZ))
    placed = (
        P(TA, None, None, GZ, None, None),
        P(TA, None, None, None, None, GZ, None),
        P(TA, None, GZ, None, None, None, None),
        P(),
        P(),
        P(),
    )
    return jax.shard_map(
        on_device,
        mesh=fine,
        in_specs=placed,
        out_specs=(P(TA, None, None, None, GZ, None), P(None, TA, None, None, None)),
        check_vma=False,
    )
```

time: 968 us -> 105 us (0.11)
  waiting for transfers between devices: 687 us -> 19 us
  matrix products: 106 us -> 0 us
  other arithmetic: 46.6 us -> 1.37 us
  local copies, waits for them, and re-layouts: 46.4 us -> 5.68 us
  blocking collectives: 51.8 us -> 20 us
  starting transfers between devices: 3.32 us -> 32.7 us
  Pallas kernels: 0 us -> 21.8 us
  between operations: 17.8 us -> 3.43 us
    psum x2 -> x0, waiting for transfers between devices: 687 us -> none  [the longest x1 645 us: from_root(): return lax.psum(kept, axis)]
    dot_general x5 -> x0, matrix products: 106 us -> none  [the longest x1 90.4 us: contraction(): lax.dot_general(sink_side, image_side, (((4, 5, 2, 7), (1, 2, 3, 7)), ((3...]
    psum x1, blocking collectives: 51.8 us -> 9.18 us  [on_device(): correlator = lax.psum(spreadout, GZ).reshape(NSRC, 1, 2, 2, 2)]
    another operation x15 -> x2, other arithmetic: 24.8 us -> 0.02 us  [the longest x1 0.01 us: on_device(): jnp.stack([lax.dynamic_index_in_dim(chunks, sources[s] >> 1, 0, keepdims=...]
    all_to_all x0 -> x3, starting transfers between devices: none -> 23.1 us  [the longest x1 9.89 us: on_device(): source_phi = lax.all_to_all(spread, YZ, 0, 0, tiled=True)]
    pallas_call x0 -> x3, Pallas kernels: none -> 21.8 us  [call(): pl.pallas_call(kernel, out_shape=outs, in_specs=[SMEM if x.ndim == 1 else...]
    all_to_all x0 -> x3, waiting for transfers between devices: none -> 17.2 us  [the longest x1 9.7 us: on_device(): source_phi = lax.all_to_all(spread, YZ, 0, 0, tiled=True)]
    dot_general x1 -> x0, local copies, waits for them, and re-layouts: 13.2 us -> none  [contraction(): lax.dot_general(peramb_slice, source_block, (((3, 5), (3, 5)), ((0,), (0,...]
  transfers between devices with their start and end apart: 4 -> 8, of which waited for: 2 -> 4; matrix products, arithmetic and copies ran while one was open for 5% -> 4% of each run, Pallas kernels for 0% -> 14%
where the time goes in v1:
time: 105 us; the launch traced here: 104 us
  starting transfers between devices  32.7 us (31%)
  Pallas kernels  21.8 us (21%)
  blocking collectives  20 us (19%)
  waiting for transfers between devices  19 us (18%)
  local copies, waits for them, and re-layouts  5.68 us (5%)
  between operations  3.43 us (3%)
  other arithmetic  1.37 us (1%)
    pallas_call x3, Pallas kernels, call(): pl.pallas_call(kernel, out_shape=outs, in_specs=[SMEM if x.ndim == 1 else...  21.8 us
    all_to_all x1, blocking collectives, on_device(): shares = lax.all_to_all(partial, GZ, 0, 0, tiled=True)  10.8 us
    all_to_all x1, starting transfers between devices, on_device(): source_phi = lax.all_to_all(spread, YZ, 0, 0, tiled=True)  9.89 us
    all_to_all x1, starting transfers between devices, on_device(): chunks = lax.all_to_all(phi.reshape(32, 8, 128), YZ, 0, 0, tiled=True)  9.89 us
    all_to_all x1, waiting for transfers between devices, on_device(): source_phi = lax.all_to_all(spread, YZ, 0, 0, tiled=True)  9.7 us
    psum x1, blocking collectives, on_device(): correlator = lax.psum(spreadout, GZ).reshape(NSRC, 1, 2, 2, 2)  9.18 us
    all_to_all x1, waiting for transfers between devices, on_device(): chunks = lax.all_to_all(phi.reshape(32, 8, 128), YZ, 0, 0, tiled=True)  4.39 us
    ppermute x3, starting transfers between devices, partner(): lax.ppermute(value, axis, [((i + distance) % n, i) for i in range(n)])  3.82 us
  transfers between devices with their start and end apart: 8, of which 4 were waited for; matrix products, arithmetic and copies ran while one was open for 4% of the time, Pallas kernels for 14%

profile of v1, /device:TPU:1, one launch (start us, length us, event | category | flops | bytes accessed | tf_op | source)
XLA Modules:
  0.0 104.0 jit_solution(9838192530395746741)
XLA Ops:
  0.7 1.5 %copy.28 = bf16[1,2,3,4,256,128]{5,4,2,1,3,0:T(8,128)(2,1)S(1)} copy(bf16[1,2,3,4,256,128]{5,4,3,2,1,0:T(8,128)(2,1)} %param.6) | data formatting | bytes 3145728 | tf_op args[0]
  2.3 3.3 %collective-permute-start = (bf16[2,3,256,128]{3,2,1,0:T(8,128)(2,1)S(1)}, bf16[2,3,256,128]{3,2,1,0:T(8,128)(2,1)S(1)}, u32[]{:S(2)}, u32[]{:S(2)}) collective-permute-start(bf16[2,3,256,128]{3,2,1,0:T(8,128)(2,1)S(1)} %slice_bitcast_fusion), channel_id=1, source_target_pairs={{1,0},{2,1},{3,2},{0,3},{5,4},{6,5},{7,6},{4,7},{9,8},{10,9},{11,1... | collective-permute-start | bytes 1179656 | tf_op jit(solution)/shard_map/ppermute | solution.py:239
  5.6 0.1 reshape.102
  5.7 0.1 reshape.103
  5.8 0.1 sin.14
  5.9 0.1 cos.14
  6.0 0.1 pad_add_fusion.ints
  6.1 0.1 copy.18
  6.2 0.1 reshape.104.shifts
  6.4 15.0 %shard_map.77 = (f32[4,512,256]{2,1,0:T(8,128)S(1)}, bf16[2,512,768]{2,1,0:T(8,128)(2,1)S(1)}) custom-call(s32[11]{0:T(128)S(1)} %pad_add_fusion.ints, bf16[2,3,4,256,128]{4,3,2,1,0:T(8,128)(2,1)S(1)} %bitcast.32, f32[4,54,256]{2,1,0:T(8,128)S(1)} %bitcast.34), custom_call_target="tpu_custom_call" | custom-call | flops 4000000000 | bytes 5000000 | tf_op jit(solution)/shard_map/pallas_call | solution.py:218
  21.4 1.9 %shard_map.78 = f32[4,2,128,128]{3,2,1,0:T(8,128)S(1)} custom-call(s32[11]{0:T(128)S(1)} %pad_add_fusion.ints, f32[12]{0:T(128)S(1)} %reshape.104.shifts, bf16[2,3,256,128]{3,2,1,0:T(8,128)(2,1)S(1)} %collective-permute-done.halo, f32[1,54,256]{2,1,0:T(8,128)S(1)} %slice.41.links, f32[4,512,256]{2,1,0:T(8,128)S(1)} %get-tuple-element.6.acc, ...), custom_call_target="tpu_custom_call" | custom-call | flops 500000000 | bytes 5000000 | tf_op jit(solution)/shard_map/pallas_call | solution.py:218
  23.3 10.8 %all_to_all.20 = f32[4,2,128,128]{3,2,1,0:T(8,128)S(1)} all-to-all(f32[4,2,128,128]{3,2,1,0:T(8,128)S(1)} %shard_map.78), channel_id=1, replica_groups=mesh['y'=4,'z'=8,'xh'=2,'xl'=2,'c'=2] {'xl','c'}, dimensions={0} | all-to-all | bytes 1048576 | tf_op jit(solution)/shard_map/all_to_all | solution.py:268
  34.2 0.6 multiply_convert_fusion.phi
  34.8 0.5 collective-permute-start.2
  35.4 9.9 %all-to-all-start.2 = ((bf16[32,8,128]{2,1,0:T(8,128)(2,1)}), bf16[32,8,128]{2,1,0:T(8,128)(2,1)S(1)}, u32[]{:S(2)}, u32[]{:S(2)}) async-start(bf16[32,8,128]{2,1,0:T(8,128)(2,1)} %bitcast.10), calls=%async_computation.2 | async-start | bytes 131072 | tf_op jit(solution)/shard_map/all_to_all | solution.py:271
  45.3 0.7 fusion.4
  48.5 1.3 %collective-permute-start.1 = (bf16[4,4,2,128,128]{4,3,2,1,0:T(8,128)(2,1)S(1)}, bf16[4,4,2,128,128]{4,3,2,1,0:T(8,128)(2,1)S(1)}, u32[]{:S(2)}, u32[]{:S(2)}) collective-permute-start(bf16[4,4,2,128,128]{4,3,2,1,0:T(8,128)(2,1)S(1)} %bitcast.36), channel_id=1, source_target_pairs={{1,0},{0,1},{3,2},{2,3},{5,4},{4,5},{7,6},{6,7},{9,8},{8,9},{11,10... | collective-permute-start | bytes 3145736 | tf_op jit(solution)/shard_map/ppermute | solution.py:231
  49.7 4.4 %all-to-all-done.2 = bf16[32,8,128]{2,1,0:T(8,128)(2,1)S(1)} async-done(((bf16[32,8,128]{2,1,0:T(8,128)(2,1)}), bf16[32,8,128]{2,1,0:T(8,128)(2,1)S(1)}, u32[]{:S(2)}, u32[]{:S(2)}) %all-to-all-start.2) | async-done | bytes 65568 | tf_op jit(solution)/shard_map/all_to_all | solution.py:271
  54.1 2.5 %collective-permute-start.4 = (bf16[4,8,128]{2,1,0:T(8,128)(2,1)S(1)}, bf16[4,8,128]{2,1,0:T(8,128)(2,1)S(1)}, u32[]{:S(2)}, u32[]{:S(2)}) collective-permute-start(bf16[4,8,128]{2,1,0:T(8,128)(2,1)S(1)} %pad_maximum_fusion), channel_id=1, source_target_pairs={{0,4},{4,0},{1,5},{5,1},{2,6},{6,2},{3,7},{7,3},{8,12},{12,8},{9,1... | collective-permute-start | bytes 24584 | tf_op jit(solution)/shard_map/ppermute | solution.py:276
  56.7 1.8 %collective-permute-done.2.tau2 = bf16[4,4,2,128,128]{4,3,2,1,0:T(8,128)(2,1)S(1)} collective-permute-done((bf16[4,4,2,128,128]{4,3,2,1,0:T(8,128)(2,1)S(1)}, bf16[4,4,2,128,128]{4,3,2,1,0:T(8,128)(2,1)S(1)}, u32[]{:S(2)}, u32[]{:S(2)}) %collective-permute-start.2) | collective-permute-done | bytes 1048608 | tf_op jit(solution)/shard_map/ppermute | solution.py:231
  58.5 2.1 %collective-permute-start.3 = (bf16[4,4,2,128,128]{4,3,2,1,0:T(8,128)(2,1)S(1)}, bf16[4,4,2,128,128]{4,3,2,1,0:T(8,128)(2,1)}, u32[]{:S(2)}, u32[]{:S(2)}) collective-permute-start(bf16[4,4,2,128,128]{4,3,2,1,0:T(8,128)(2,1)S(1)} %collective-permute-done.2.tau2), channel_id=1, source_target_pairs={{1,0},{0,1},{3,2},{2,3},{5,4},{4,5},{7,6},{6,7},{9,8},{8,9},{11,10... | collective-permute-start | bytes 3145736 | tf_op jit(solution)/shard_map/ppermute | solution.py:231
  60.5 1.5 %copy.30 = bf16[2,4,32,128]{3,2,0,1:T(8,128)(2,1)} copy(bf16[2,4,32,128]{3,2,1,0:T(8,128)(2,1)} %bitcast.6) | data formatting | bytes 131072 | tf_op jit(solution)/shard_map/convert_element_type | solution.py:269
  62.0 3.3 %all-to-all-start.1 = ((bf16[4,2,32,128]{3,2,1,0:T(8,128)(2,1)}), bf16[4,2,32,128]{3,2,1,0:T(8,128)(2,1)S(1)}, u32[]{:S(2)}, u32[]{:S(2)}) async-start(bf16[4,2,32,128]{3,2,1,0:T(8,128)(2,1)} %bitcast.30), calls=%async_computation.1 | async-start | bytes 131072 | tf_op jit(solution)/shard_map/all_to_all | solution.py:302
  65.3 3.1 %all-to-all-done.1 = bf16[4,2,32,128]{3,2,1,0:T(8,128)(2,1)S(1)} async-done(((bf16[4,2,32,128]{3,2,1,0:T(8,128)(2,1)}), bf16[4,2,32,128]{3,2,1,0:T(8,128)(2,1)S(1)}, u32[]{:S(2)}, u32[]{:S(2)}) %all-to-all-start.1) | async-done | bytes 65568 | tf_op jit(solution)/shard_map/all_to_all | solution.py:302
  68.5 0.7 broadcast_in_dim.43
  69.2 9.9 %all-to-all-start.3 = ((bf16[32,4,8,128]{3,2,1,0:T(8,128)(2,1)}), bf16[32,4,8,128]{3,2,1,0:T(8,128)(2,1)S(1)}, u32[]{:S(2)}, u32[]{:S(2)}) async-start(bf16[32,4,8,128]{3,2,1,0:T(8,128)(2,1)} %broadcast_in_dim.43), calls=%async_computation.3 | async-start | bytes 524288 | tf_op jit(solution)/shard_map/all_to_all | solution.py:279
  79.2 9.7 %all-to-all-done.3 = bf16[32,4,8,128]{3,2,1,0:T(8,128)(2,1)S(1)} async-done(((bf16[32,4,8,128]{3,2,1,0:T(8,128)(2,1)}), bf16[32,4,8,128]{3,2,1,0:T(8,128)(2,1)S(1)}, u32[]{:S(2)}, u32[]{:S(2)}) %all-to-all-start.3) | async-done | bytes 262176 | tf_op jit(solution)/shard_map/all_to_all | solution.py:279
  89.0 4.9 %shard_map.79 = f32[4,2,128,128]{3,2,1,0:T(8,128)S(1)} custom-call(bf16[2,128,128]{2,1,0:T(8,128)(2,1)} %multiply_convert_fusion.phi, bf16[4,4,2,128,128]{4,3,2,1,0:T(8,128)(2,1)S(1)} %bitcast.37, bf16[4,4,2,128,128]{4,3,2,1,0:T(8,128)(2,1)S(1)} %collective-permute-done.1.tau1, bf16[4,4,2,128,128]{4,3,2,1,0:T(8,128)(2,1)S(1)} %collective-permute-done.2.tau2, ...), custom_call_target="tpu_custom_call" | custom-call | flops 2000000000 | bytes 5000000 | tf_op jit(solution)/shard_map/pallas_call | solution.py:218
  93.8 0.1 fusion.1
  94.0 0.2 multiply_reduce_fusion
  94.2 9.2 %psum.7 = f32[4,1,2,2,2]{0,4,3,2,1:T(2,128)} all-reduce(f32[4,1,2,2,2]{0,4,3,2,1:T(2,128)S(1)} %bitcast.42), channel_id=1, replica_groups=mesh['y'=4,'z'=8,'xh'=2,'xl'=2,'c'=2] {'xl','c'}, use_global_device_ids=true, to_apply=%region_3.4 | all-reduce | flops 32 | bytes 256 | tf_op jit(solution)/shard_map/psum | solution.py:300
  103.4 0.6 copy.32
  (32 shorter events, 0.5 us)
Async XLA Ops:
  0.6 5.0 %copy-start.4 = (s32[2,3]{1,0:T(2,128)S(1)}, s32[2,3]{1,0:T(2,128)}, u32[]{:S(2)}) copy-start(s32[2,3]{1,0:T(2,128)} %param.9) | copy-start | bytes 76
  0.6 5.1 %copy-start.5 = (s32[2,2]{1,0:T(2,128)S(1)}, s32[2,2]{1,0:T(2,128)}, u32[]{:S(2)}) copy-start(s32[2,2]{1,0:T(2,128)} %param.10) | copy-start | bytes 52
  0.7 5.3 %copy-start.2 = (bf16[1,3,3,3,2,4,256]{6,5,4,3,2,1,0:T(4,128)(2,1)S(1)}, bf16[1,3,3,3,2,4,256]{6,5,4,3,2,1,0:T(4,128)(2,1)}, u32[]{:S(2)}) copy-start(bf16[1,3,3,3,2,4,256]{6,5,4,3,2,1,0:T(4,128)(2,1)} %param.7) | copy-start | bytes 331780
  2.2 4.1 %copy-start = (bf16[1,2,3,4,256,128]{5,4,3,2,1,0:T(8,128)(2,1)S(1)}, bf16[1,2,3,4,256,128]{5,4,3,2,1,0:T(8,128)(2,1)}, u32[]{:S(2)}) copy-start(bf16[1,2,3,4,256,128]{5,4,3,2,1,0:T(8,128)(2,1)} %param.6) | copy-start | bytes 4718596
  2.3 19.1 %collective-permute-start = (bf16[2,3,256,128]{3,2,1,0:T(8,128)(2,1)S(1)}, bf16[2,3,256,128]{3,2,1,0:T(8,128)(2,1)S(1)}, u32[]{:S(2)}, u32[]{:S(2)}) collective-permute-start(bf16[2,3,256,128]{3,2,1,0:T(8,128)(2,1)S(1)} %slice_bitcast_fusion), channel_id=1, source_target_pairs={{1,0},{2,1},{3,2},{0,3},{5,4},{6,5},{7,6},{4,7},{9,8},{10,9},{11,1... | collective-permute-start | bytes 1179656 | tf_op jit(solution)/shard_map/ppermute | solution.py:239
  23.3 11.6 %copy-start.1 = (bf16[1,4,1,4,2,128,128]{6,5,4,3,2,1,0:T(8,128)(2,1)S(1)}, bf16[1,4,1,4,2,128,128]{6,5,4,3,2,1,0:T(8,128)(2,1)}, u32[]{:S(2)}) copy-start(bf16[1,4,1,4,2,128,128]{6,5,4,3,2,1,0:T(8,128)(2,1)} %param.8) | copy-start | bytes 3145732
  23.3 21.9 %copy-start.3 = (s32[4]{0:T(128)S(1)}, s32[4]{0:T(128)}, u32[]{:S(2)}) copy-start(s32[4]{0:T(128)} %param.11) | copy-start | bytes 52
  34.8 23.6 %collective-permute-start.2 = (bf16[4,4,2,128,128]{4,3,2,1,0:T(8,128)(2,1)S(1)}, bf16[4,4,2,128,128]{4,3,2,1,0:T(8,128)(2,1)S(1)}, u32[]{:S(2)}, u32[]{:S(2)}) collective-permute-start(bf16[4,4,2,128,128]{4,3,2,1,0:T(8,128)(2,1)S(1)} %bitcast.35), channel_id=1, source_target_pairs={{2,0},{0,2},{3,1},{1,3},{6,4},{4,6},{7,5},{5,7},{10,8},{8,10},{11,... | collective-permute-start | bytes 3145736 | tf_op jit(solution)/shard_map/ppermute | solution.py:231
  35.4 18.8 %all-to-all-start.2 = ((bf16[32,8,128]{2,1,0:T(8,128)(2,1)}), bf16[32,8,128]{2,1,0:T(8,128)(2,1)S(1)}, u32[]{:S(2)}, u32[]{:S(2)}) async-start(bf16[32,8,128]{2,1,0:T(8,128)(2,1)} %bitcast.10), calls=%async_computation.2 | async-start | bytes 131072 | tf_op jit(solution)/shard_map/all_to_all | solution.py:271
  48.5 40.5 %collective-permute-start.1 = (bf16[4,4,2,128,128]{4,3,2,1,0:T(8,128)(2,1)S(1)}, bf16[4,4,2,128,128]{4,3,2,1,0:T(8,128)(2,1)S(1)}, u32[]{:S(2)}, u32[]{:S(2)}) collective-permute-start(bf16[4,4,2,128,128]{4,3,2,1,0:T(8,128)(2,1)S(1)} %bitcast.36), channel_id=1, source_target_pairs={{1,0},{0,1},{3,2},{2,3},{5,4},{4,5},{7,6},{6,7},{9,8},{8,9},{11,10... | collective-permute-start | bytes 3145736 | tf_op jit(solution)/shard_map/ppermute | solution.py:231
  54.1 11.1 %collective-permute-start.4 = (bf16[4,8,128]{2,1,0:T(8,128)(2,1)S(1)}, bf16[4,8,128]{2,1,0:T(8,128)(2,1)S(1)}, u32[]{:S(2)}, u32[]{:S(2)}) collective-permute-start(bf16[4,8,128]{2,1,0:T(8,128)(2,1)S(1)} %pad_maximum_fusion), channel_id=1, source_target_pairs={{0,4},{4,0},{1,5},{5,1},{2,6},{6,2},{3,7},{7,3},{8,12},{12,8},{9,1... | collective-permute-start | bytes 24584 | tf_op jit(solution)/shard_map/ppermute | solution.py:276
  58.5 30.5 %collective-permute-start.3 = (bf16[4,4,2,128,128]{4,3,2,1,0:T(8,128)(2,1)S(1)}, bf16[4,4,2,128,128]{4,3,2,1,0:T(8,128)(2,1)}, u32[]{:S(2)}, u32[]{:S(2)}) collective-permute-start(bf16[4,4,2,128,128]{4,3,2,1,0:T(8,128)(2,1)S(1)} %collective-permute-done.2.tau2), channel_id=1, source_target_pairs={{1,0},{0,1},{3,2},{2,3},{5,4},{4,5},{7,6},{6,7},{9,8},{8,9},{11,10... | collective-permute-start | bytes 3145736 | tf_op jit(solution)/shard_map/ppermute | solution.py:231
  62.0 6.5 %all-to-all-start.1 = ((bf16[4,2,32,128]{3,2,1,0:T(8,128)(2,1)}), bf16[4,2,32,128]{3,2,1,0:T(8,128)(2,1)S(1)}, u32[]{:S(2)}, u32[]{:S(2)}) async-start(bf16[4,2,32,128]{3,2,1,0:T(8,128)(2,1)} %bitcast.30), calls=%async_computation.1 | async-start | bytes 131072 | tf_op jit(solution)/shard_map/all_to_all | solution.py:302
  69.2 19.6 %all-to-all-start.3 = ((bf16[32,4,8,128]{3,2,1,0:T(8,128)(2,1)}), bf16[32,4,8,128]{3,2,1,0:T(8,128)(2,1)S(1)}, u32[]{:S(2)}, u32[]{:S(2)}) async-start(bf16[32,4,8,128]{3,2,1,0:T(8,128)(2,1)} %broadcast_in_dim.43), calls=%async_computation.3 | async-start | bytes 524288 | tf_op jit(solution)/shard_map/all_to_all | solution.py:279

commit v2 on v1

v2 whole, which is shorter than its diff:
```python
import functools
import math

import jax
import jax.numpy as jnp
import numpy as np
from jax import lax
from jax.experimental import pallas as pl
from jax.experimental.pallas import tpu as pltpu
from jax.sharding import Mesh
from jax.sharding import PartitionSpec as P

LX = 16
LY = 16
NSRC = 4
BF = jnp.bfloat16
F32 = jnp.float32
NT_DIMS = (((1,), (1,)), ((), ()))
TA = ("y", "z", "xh")
YZ = ("y", "z")
GZ = ("xl", "c")


def dot_nt(a, b):
    return lax.dot_general(a, b, NT_DIMS, preferred_element_type=F32)


def dot_nn(a, b):
    return jnp.dot(a, b, preferred_element_type=F32)


def shift_matrix(direction):
    row = lax.broadcasted_iota(jnp.int32, (256, 256), 0)
    col = lax.broadcasted_iota(jnp.int32, (256, 256), 1)
    if direction == 0:
        target = (col + LY) & 255
    else:
        target = (col & ~(LY - 1)) | ((col + 1) & (LY - 1))
    return jnp.where(row == target, 1.0, 0.0).astype(F32).astype(BF)


def unit_matrix(n):
    row = lax.broadcasted_iota(jnp.int32, (n, n), 0)
    col = lax.broadcasted_iota(jnp.int32, (n, n), 1)
    return jnp.where(row == col, 1.0, 0.0).astype(F32).astype(BF)


def transport(links, z, direction, source, target):
    for half in range(2):
        lanes = pl.ds(half * 128, 128)
        coef = [
            [
                [
                    jnp.broadcast_to(
                        links[z, pl.ds(direction * 18 + a * 6 + b * 2 + part, 1), lanes], (8, 128)
                    )
                    for part in range(2)
                ]
                for b in range(3)
            ]
            for a in range(3)
        ]

        for step in range(8):
            parts = []
            for sub in range(2):
                at = pl.ds(step * 16 + sub * 8, 8)
                vec = [[source(part * 3 + b, at, lanes) for b in range(3)] for part in range(2)]
                out = []
                for a in range(3):
                    re = im = None
                    for b in range(3):
                        ur, ui = coef[a][b]
                        tr = ur * vec[0][b] - ui * vec[1][b]
                        ti = ur * vec[1][b] + ui * vec[0][b]
                        re = tr if re is None else re + tr
                        im = ti if im is None else im + ti
                    out.append((re, im))
                parts.append(out)
            for a in range(3):
                for part in range(2):
                    block = jnp.concatenate([parts[0][a][part], parts[1][a][part]], axis=0)
                    start = part * 128 + step * 16
                    target[pl.ds(start, 16), pl.ds(a * 256 + half * 128, 128)] = block.astype(BF)


def phase_rows(ints, row, plane):
    site = lax.broadcasted_iota(jnp.int32, (8, 256), 1)
    x1 = site >> 4
    x2 = site & (LY - 1)
    steps = ints[row * 3] * x1 + ints[row * 3 + 1] * x2 + ints[row * 3 + 2] * plane
    angle = (steps & 15).astype(F32) * (2.0 * math.pi / 16.0)
    return jnp.cos(angle), jnp.sin(angle)


def phase_plane(ints, z, vt, phased):
    for m in range(2):
        cosine, sine = phase_rows(ints, m, ints[10] + z)
        for half in range(2):
            lanes = pl.ds(half * 128, 128)
            cs = cosine[:, half * 128 : half * 128 + 128]
            sn = sine[:, half * 128 : half * 128 + 128]
            cs = jnp.concatenate([cs] * 2, axis=0)
            sn = jnp.concatenate([sn] * 2, axis=0)
            for step in range(8):
                at = pl.ds(step * 16, 16)
                for a in range(3):
                    re = vt[z, a, at, lanes]
                    im = vt[z, 3 + a, at, lanes]
                    rc, rs, ic, js = re * cs, re * sn, im * cs, im * sn
                    to = pl.ds(a * 256 + half * 128, 128)
                    for block, value in enumerate((rc - js, -(rs + ic), rc + js, rs - ic)):
                        phased[m, pl.ds(block * 128 + step * 16, 16), to] = value.astype(BF)


def local_kernel(ints, eig, narrow, acc, phased, edge_links, vt, vs, field, perm, links):
    unit = unit_matrix(128)
    perm[0] = shift_matrix(0)
    perm[1] = shift_matrix(1)
    wide = narrow[...].astype(F32)
    for z in range(4):
        links[z] = wide[:, z, :]
    edge_links[0] = links[3]

    def load(z, _):
        for comp in range(6):
            vt[z, comp] = dot_nt(unit, eig[comp // 3, comp % 3, z])
        return 0
    lax.fori_loop(0, 4, load, 0)
    acc[...] = jnp.zeros_like(acc)
    which = [jnp.where(ints[6 + 2 * m] == 3, ints[7 + 2 * m], ints[6 + 2 * m]) - 1 for m in range(2)]
    def plane(z, last):
        phase_plane(ints, z, vt, phased)
        for direction in range(2):
            vs[direction] = dot_nn(vt[z].reshape(768, 256).astype(BF), perm[direction]).reshape(6, 128, 256)
        for direction in range(2):
            transport(links, z, direction, lambda comp, at, lanes: vs[direction, comp, at, lanes], field.at[direction])
        if not last:
            transport(links, z, 2, lambda comp, at, lanes: vt[z + 1, comp, at, lanes], field.at[2])
            t = dot_nt(phased[...].reshape(1024, 768), field[2])
            acc[0] += t[:512]
            acc[2] += t[512:]
        for m in range(2):
            acc[2 * m + 1] += dot_nt(phased[m], field[which[m]])
        return 0
    lax.fori_loop(0, 3, lambda z, _: plane(z, False), 0)
    plane(3, True)


def edge_kernel(ints, halo, links, acc, phased, tau, keep, send, rest, vt, field):
    unit = unit_matrix(128)
    for comp in range(6):
        vt[comp] = dot_nt(unit, halo[comp // 3, comp % 3])
    transport(links, 0, 2, lambda comp, at, lanes: vt[comp, at, lanes], field)
    rest[...] = tau[1:4]
    core = ints[11] & 1
    edge = dot_nt(phased[...].reshape(1024, 768), field[...])
    for m in range(2):
        along = jnp.where(ints[6 + 2 * m] == 3, 0, 1)
        for o in range(2):
            t = acc[2 * m + o]
            if o == 0:
                t = t + edge[512 * m : 512 * m + 512]
                slot = along
            else:
                slot = 1 - along
            direction = ints[6 + 2 * m + slot] - 1
            turn = jnp.full((8, 128), ints[3 * m + direction] & 15, jnp.int32).astype(F32)
            turn = turn * (2.0 * math.pi / 16.0)
            cd = jnp.cos(turn)[:1]
            sd = jnp.sin(turn)[:1]
            ar = t[0:128, 0:128] - t[128:256, 128:256]
            ai = t[0:128, 128:256] + t[128:256, 0:128]
            br = (t[256:384, 0:128] - t[384:512, 128:256]).T
            bi = (t[256:384, 128:256] + t[384:512, 0:128]).T
            re = ar - cd * br + sd * bi
            im = ai + sd * br + cd * bi

            def store(ref, m=m, re=re, im=im):
                ref[m, 0] = re
                ref[m, 1] = im

            pl.when(slot == core)(functools.partial(store, keep))
            pl.when(slot != core)(functools.partial(store, send))


def pieces_kernel(eig, tau, lowest, head, sems):
    moves = [(eig.at[part, a, 0], lowest.at[part, a]) for part in range(2) for a in range(3)]
    moves.append((tau.at[pl.ds(0, 1)], head))
    copies = [pltpu.make_async_copy(*move, sems.at[n]) for n, move in enumerate(moves)]
    for copy in copies:
        copy.start()
    for copy in copies:
        copy.wait()


def table_kernel(ints, pair0, pair1, pair2, pair3, table):
    lane = lax.broadcasted_iota(jnp.int32, (8, 128), 1)
    total = jnp.zeros((8, 128), F32)
    for d, got in enumerate((pair0, pair1, pair2, pair3)):
        total = jnp.where(lane == ((ints[11] + 4 - d) & 3), got[...], total)
    table[...] = total


def half_kernel(ints, keep, got, mine, other):
    chip = ints[11] >> 1
    mine[...] = keep[chip] + got[chip]
    other[...] = (keep[1 - chip] + got[1 - chip]).astype(BF)


def phi_kernel(ints, mine, got, phi, row0, row1, row2, row3):
    phi[...] = ((mine[...] + got[...].astype(F32)) * (1.0 / math.sqrt(12.0 * LX * LY * 16))).astype(BF)
    for d, out in enumerate((row0, row1, row2, row3)):
        rows = pl.ds(pl.multiple_of(((ints[11] + d) & 3) * 32, 32), 32)
        for part in range(2):
            out[part] = phi[part, rows, :]


def pick_kernel(sources, chunks, out):
    for s in range(NSRC):
        out[s] = chunks[sources[s] >> 1]


def spread_kernel(ints, sources, mine, other, out):
    for s in range(NSRC):
        value = jnp.where((sources[s] & 1) == ints[12], mine[s], other[s])
        for place in range(32):
            out[place, s] = value


def loop_kernel(phi, whole, *refs, start):
    first = jnp.concatenate(
        [
            jnp.concatenate([phi[0], phi[1]], axis=1),
            jnp.concatenate([phi[1], -phi[0]], axis=1),
        ],
        axis=0,
    )
    out = refs[-1]
    for s in range(NSRC):
        piece, at = (0, 0) if s == 0 else (1, s - 1)
        taus = [(ref, at) for ref in refs[piece:-1:2]]
        if start:
            total = jnp.zeros((128, 256), F32)
            taus.append((whole, s))
        else:
            total = jnp.concatenate([whole[s, 0], whole[s, 1]], axis=1)
        for tau, at in taus:
            pairs = [(tau[at, beta, 0], tau[at, beta, 1]) for beta in range(4)]
            left = jnp.concatenate([jnp.concatenate(pair, axis=0) for pair in pairs], axis=1)
            mid = lax.dot_general(
                left, first, (((0,), (0,)), ((), ())), preferred_element_type=F32
            ).astype(BF)
            mid = jnp.concatenate([mid[beta * 128 : beta * 128 + 128] for beta in range(4)], axis=1)
            second = jnp.concatenate(
                [
                    jnp.concatenate(row, axis=1)
                    for tr, ti in pairs
                    for row in ((tr, ti), (-ti, tr))
                ],
                axis=0,
            )
            total = total + dot_nn(mid, second)
        out[s, 0] = total[:, :128]
        out[s, 1] = total[:, 128:]


def close_kernel(ints, looped, spread, row0, row1, row2, row3, rows, pair):
    for d, got in enumerate((row0, row1, row2, row3)):
        rows[(ints[11] + 4 - d) & 3] = got[...]
    for s in range(NSRC):
        src_re = spread[0:16, s].astype(F32).reshape(128, 128)
        src_im = spread[16:32, s].astype(F32).reshape(128, 128)
        yr, yi = looped[s, 0], looped[s, 1]
        re = jnp.sum(yr * src_re + yi * src_im) * (1.0 / (8.0 * 128))
        im = jnp.sum(yi * src_re - yr * src_im) * (1.0 / (8.0 * 128))
        pair[2 * s : 2 * s + 1, :] = jnp.full((1, 128), re, F32)
        pair[2 * s + 1 : 2 * s + 2, :] = jnp.full((1, 128), im, F32)


VMEM = pl.BlockSpec(memory_space=pltpu.VMEM)
SMEM = pl.BlockSpec(memory_space=pltpu.SMEM)


def call(kernel, outs, inputs, scratch, flops, moved):
    return pl.pallas_call(
        kernel,
        out_shape=outs,
        in_specs=[SMEM if x.ndim == 1 else VMEM for x in inputs],
        out_specs=jax.tree.map(lambda _: VMEM, outs),
        scratch_shapes=scratch,
        compiler_params=pltpu.CompilerParams(vmem_limit_bytes=40 * 2**20),
        cost_estimate=pl.CostEstimate(flops=flops, bytes_accessed=moved, transcendentals=0),
    )(*inputs)


def partner(value, axis, distance=1):
    n = math.prod(lax.axis_size(name) for name in ([axis] if isinstance(axis, str) else axis))
    return lax.ppermute(value, axis, [((i + distance) % n, i) for i in range(n)])


def shaped(*shape, dtype=F32):
    return jax.ShapeDtypeStruct(shape, dtype)


def on_device(eigvecs, gauge_links, peramb, momenta, disp_paths, sources):
    eig = eigvecs[0]
    depth = eig.shape[2]
    own = lax.axis_index("xl") * 2 + lax.axis_index("c")
    tau = peramb[0, :, 0]
    piece = [shaped(n, *tau.shape[1:], dtype=BF) for n in (1, 3)]
    lowest, head = pl.pallas_call(
        pieces_kernel,
        out_shape=(shaped(2, 3, 256, 128, dtype=BF), piece[0]),
        in_specs=[pl.BlockSpec(memory_space=pl.ANY)] * 2,
        out_specs=(VMEM,) * 2,
        scratch_shapes=[pltpu.SemaphoreType.DMA((7,))],
    )(eig, tau)
    halo = partner(lowest, GZ)
    near = partner(tau, "c")
    far = [partner(head, "xl")]
    links = gauge_links[0].reshape(54, depth, LX * LY)
    ints = jnp.concatenate(
        [
            momenta.reshape(6),
            disp_paths.reshape(4),
            jnp.stack([own * depth, own, lax.axis_index("xh")]).astype(jnp.int32),
        ]
    )
    acc, phased, edge_links = call(
        local_kernel,
        (shaped(4, 512, 256), shaped(2, 512, 768, dtype=BF), shaped(1, 54, 256)),
        (ints, eig, links),
        [
            pltpu.VMEM((4, 6, 128, 256), F32),
            pltpu.VMEM((2, 6, 128, 256), F32),
            pltpu.VMEM((3, 256, 768), BF),
            pltpu.VMEM((2, 256, 256), BF),
            pltpu.VMEM((depth, 54, 256), F32),
        ],
        4 * 10**9,
        5 * 10**6,
    )
    far[0], acc = lax.optimization_barrier((far[0], acc))
    keep, send, rest = call(
        edge_kernel,
        (shaped(2, 2, 128, 128), shaped(2, 2, 128, 128), piece[1]),
        (ints, halo, edge_links, acc, phased, tau),
        [pltpu.VMEM((6, 128, 256), F32), pltpu.VMEM((256, 768), BF)],
        5 * 10**8,
        5 * 10**6,
    )
    whole = shaped(2, 128, 128)
    mine, other = call(half_kernel, (whole, shaped(2, 128, 128, dtype=BF)), (ints, keep, partner(send, "c")), [], 10**5, 10**6)
    arrived = partner(other, "xl")
    last, arrived = lax.optimization_barrier((rest, arrived))
    far.append(partner(last, "xl"))
    block = shaped(2, 32, 128, dtype=BF)
    phi, *rows = call(
        phi_kernel,
        (shaped(2, 128, 128, dtype=BF), block, block, block, block),
        (ints, mine, arrived),
        [],
        10**5,
        10**6,
    )

    chunks = lax.all_to_all(phi.reshape(32, 8, 128), YZ, 0, 0, tiled=True)
    four = shaped(NSRC, 8, 128, dtype=BF)
    picked = call(pick_kernel, four, (sources, chunks), [], 10**4, 10**5)
    crossed = partner(picked, "xh")
    phi, _, far, rows = lax.optimization_barrier((phi, picked, far, rows))
    diagonal = [partner(piece, "c") for piece in far]
    rows = rows[:1] + [partner(row, GZ, -d) for d, row in enumerate(rows) if d]
    looped = shaped(NSRC, 2, 128, 128)
    partly = call(
        functools.partial(loop_kernel, start=True),
        looped,
        (phi, near, head, rest, *far),
        [],
        15 * 10**8,
        4 * 10**6,
    )
    looped = call(
        functools.partial(loop_kernel, start=False),
        looped,
        (phi, partly, *diagonal),
        [],
        5 * 10**8,
        2 * 10**6,
    )
    looped, crossed, *rows = lax.optimization_barrier((looped, crossed, *rows))
    spread = call(
        spread_kernel,
        shaped(32, NSRC, 8, 128, dtype=BF),
        (ints, sources, picked, crossed),
        [],
        10**4,
        10**5,
    )
    spread = lax.all_to_all(spread, YZ, 0, 0, tiled=True)
    rows, pair = call(
        close_kernel,
        (shaped(4, 2, 32, 128, dtype=BF), shaped(8, 128)),
        (ints, looped, spread, *rows),
        [],
        10**5,
        10**6,
    )
    pairs = [pair] + [partner(pair, GZ, -d) for d in range(1, 4)]
    table = call(table_kernel, shaped(8, 128), (ints, *pairs), [], 10**3, 10**4)
    correlator = jnp.swapaxes(table[:, :4].reshape(NSRC, 2, 4), 1, 2)
    return rows.reshape(1, 2, 2, 2, 32, 128), correlator.reshape(NSRC, 1, 2, 2, 2)


def solution(mesh):
    fine = Mesh(np.asarray(mesh.devices).reshape(4, 8, 2, 2, 2), (*TA, *GZ))
    placed = (
        P(TA, None, None, GZ, None, None),
        P(TA, None, None, None, None, GZ, None),
        P(TA, None, GZ, None, None, None, None),
        P(),
        P(),
        P(),
    )
    return jax.shard_map(
        on_device,
        mesh=fine,
        in_specs=placed,
        out_specs=(P(TA, None, None, None, GZ, None), P(None, TA, None, None, None)),
        check_vma=False,
    )
```

time: 105 us -> 84.9 us (0.81)
  blocking collectives: 20 us -> 34.6 us
  starting transfers between devices: 32.7 us -> 19.7 us
  waiting for transfers between devices: 19 us -> 6.47 us
  local copies, waits for them, and re-layouts: 5.68 us -> 0.96 us
  between operations: 3.43 us -> 0.85 us
  other arithmetic: 1.37 us -> 0 us
    all_to_all x1 -> x2, blocking collectives: 10.8 us -> 34.6 us  [the longest x1 19.2 us: on_device(): chunks = lax.all_to_all(phi.reshape(32, 8, 128), YZ, 0, 0, tiled=True)]
    all_to_all x3 -> x0, starting transfers between devices: 23.1 us -> none  [the longest x1 9.89 us: on_device(): source_phi = lax.all_to_all(spread, YZ, 0, 0, tiled=True)]
    all_to_all x3 -> x0, waiting for transfers between devices: 17.2 us -> none  [the longest x1 9.7 us: on_device(): source_phi = lax.all_to_all(spread, YZ, 0, 0, tiled=True)]
    ppermute x3 -> x15, starting transfers between devices: 3.82 us -> 19.7 us  [partner(): lax.ppermute(value, axis, [((i + distance) % n, i) for i in range(n)])]
    psum x1 -> x0, blocking collectives: 9.18 us -> none  [on_device(): correlator = lax.psum(spreadout, GZ).reshape(NSRC, 1, 2, 2, 2)]
    ppermute x2 -> x0, starting transfers between devices: 5.86 us -> none  [the longest x1 3.32 us: on_device(): halo = lax.ppermute(halo_out, GZ, [((i + 1) % 4, i) for i in range(4)])]
    ppermute x3 -> x15, waiting for transfers between devices: 1.79 us -> 6.47 us  [partner(): lax.ppermute(value, axis, [((i + distance) % n, i) for i in range(n)])]
    unnamed x14, local copies, waits for them, and re-layouts: 2.21 us -> 0.03 us
  transfers between devices with their start and end apart: 8 -> 15, of which waited for: 4 -> 4; matrix products, arithmetic and copies ran while one was open for 4% -> 0% of each run, Pallas kernels for 14% -> 17%
where the time goes in v2:
time: 84.9 us; the launch traced here: 84.7 us
  blocking collectives  34.6 us (41%)
  Pallas kernels  22.1 us (26%)
  starting transfers between devices  19.7 us (23%)
  waiting for transfers between devices  6.47 us (8%)
  local copies, waits for them, and re-layouts  0.96 us (1%)
  between operations  0.85 us (1%)
    pallas_call x10, Pallas kernels, call(): pl.pallas_call(kernel, out_shape=outs, in_specs=[SMEM if x.ndim == 1 else...  19.9 us
    ppermute x15, starting transfers between devices, partner(): lax.ppermute(value, axis, [((i + distance) % n, i) for i in range(n)])  19.7 us
    all_to_all x1, blocking collectives, on_device(): chunks = lax.all_to_all(phi.reshape(32, 8, 128), YZ, 0, 0, tiled=True)  19.2 us
    all_to_all x1, blocking collectives, on_device(): spread = lax.all_to_all(spread, YZ, 0, 0, tiled=True)  15.4 us
    ppermute x15, waiting for transfers between devices, partner(): lax.ppermute(value, axis, [((i + distance) % n, i) for i in range(n)])  6.47 us
    pallas_call x1, Pallas kernels, on_device(): pl.pallas_call(pieces_kernel, out_shape=(shaped(2, 3, 256, 128, dtype=BF)...  2.17 us
  transfers between devices with their start and end apart: 15, of which 4 were waited for; matrix products, arithmetic and copies ran while one was open for 0% of the time, Pallas kernels for 17%

profile of v2, /device:TPU:1, one launch (start us, length us, event | category | flops | bytes accessed | tf_op | source)
XLA Modules:
  0.0 84.7 jit_solution(2697081768577404995)
XLA Ops:
  0.7 2.2 %shard_map.77 = (bf16[2,3,256,128]{3,2,1,0:T(8,128)(2,1)}, bf16[1,4,2,128,128]{4,3,2,1,0:T(8,128)(2,1)}) custom-call(bf16[2,3,4,256,128]{4,3,2,1,0:T(8,128)(2,1)} %bitcast.16, bf16[4,4,2,128,128]{4,3,2,1,0:T(8,128)(2,1)} %bitcast.13), custom_call_target="tpu_custom_call" | custom-call | tf_op jit(solution)/shard_map/pallas_call | solution.py:312
  2.8 3.3 %collective-permute-start = (bf16[2,3,256,128]{3,2,1,0:T(8,128)(2,1)}, bf16[2,3,256,128]{3,2,1,0:T(8,128)(2,1)S(1)}, u32[]{:S(2)}, u32[]{:S(2)}) collective-permute-start(bf16[2,3,256,128]{3,2,1,0:T(8,128)(2,1)} %get-tuple-element.36), channel_id=1, source_target_pairs={{1,0},{2,1},{3,2},{0,3},{5,4},{6,5},{7,6},{4,7},{9,8},{10,9},{11,1... | collective-permute-start | bytes 1179656 | tf_op jit(solution)/shard_map/ppermute | solution.py:299
  6.2 0.1 reshape.22
  6.3 0.1 concatenate.3.ints
  6.4 10.7 %shard_map.78 = (f32[4,512,256]{2,1,0:T(8,128)S(1)}, bf16[2,512,768]{2,1,0:T(8,128)(2,1)S(1)}, f32[1,54,256]{2,1,0:T(8,128)S(1)}) custom-call(s32[13]{0:T(128)S(1)} %concatenate.3.ints, bf16[2,3,4,256,128]{4,3,2,1,0:T(8,128)(2,1)S(1)} %bitcast.17, bf16[54,4,256]{2,1,0:T(4,128)(2,1)S(1)} %bitcast.20), custom_call_target="tpu_custom_call" | custom-call | flops 4000000000 | bytes 5000000 | tf_op jit(solution)/shard_map/pallas_call | solution.py:286
  17.2 2.1 %shard_map.79 = (f32[2,2,128,128]{3,2,1,0:T(8,128)S(1)}, f32[2,2,128,128]{3,2,1,0:T(8,128)S(1)}, bf16[3,4,2,128,128]{4,3,2,1,0:T(8,128)(2,1)S(1)}) custom-call(s32[13]{0:T(128)S(1)} %concatenate.3.ints, bf16[2,3,256,128]{3,2,1,0:T(8,128)(2,1)S(1)} %collective-permute-done.halo, f32[1,54,256]{2,1,0:T(8,128)S(1)} %get-tuple-element.37.links, ...), custom_call_target="tpu_custom_call" | custom-call | flops 500000000 | bytes 5000000 | tf_op jit(solution)/shard_map/pallas_call | solution.py:286
  19.4 0.4 collective-permute-start.2
  19.7 1.2 %collective-permute-done.2.got = f32[2,2,128,128]{3,2,1,0:T(8,128)S(1)} collective-permute-done((f32[2,2,128,128]{3,2,1,0:T(8,128)S(1)}, f32[2,2,128,128]{3,2,1,0:T(8,128)S(1)}, u32[]{:S(2)}, u32[]{:S(2)}) %collective-permute-start.2) | collective-permute-done | bytes 262176 | tf_op jit(solution)/shard_map/ppermute | solution.py:299
  21.0 0.6 shard_map.80
  21.6 1.8 %collective-permute-start.3 = (bf16[2,128,128]{2,1,0:T(8,128)(2,1)S(1)}, bf16[2,128,128]{2,1,0:T(8,128)(2,1)S(1)}, u32[]{:S(2)}, u32[]{:S(2)}) collective-permute-start(bf16[2,128,128]{2,1,0:T(8,128)(2,1)S(1)} %get-tuple-element.46), channel_id=1, source_target_pairs={{2,0},{0,2},{3,1},{1,3},{6,4},{4,6},{7,5},{5,7},{10,8},{8,10},{11,... | collective-permute-start | bytes 196616 | tf_op jit(solution)/shard_map/ppermute | solution.py:299
  23.4 2.2 %collective-permute-done.3.got = bf16[2,128,128]{2,1,0:T(8,128)(2,1)S(1)} collective-permute-done((bf16[2,128,128]{2,1,0:T(8,128)(2,1)S(1)}, bf16[2,128,128]{2,1,0:T(8,128)(2,1)S(1)}, u32[]{:S(2)}, u32[]{:S(2)}) %collective-permute-start.3) | collective-permute-done | bytes 65568 | tf_op jit(solution)/shard_map/ppermute | solution.py:299
  25.5 1.0 %collective-permute-start.4 = (bf16[3,4,2,128,128]{4,3,2,1,0:T(8,128)(2,1)S(1)}, bf16[3,4,2,128,128]{4,3,2,1,0:T(8,128)(2,1)S(1)}, u32[]{:S(2)}, u32[]{:S(2)}) collective-permute-start(bf16[3,4,2,128,128]{4,3,2,1,0:T(8,128)(2,1)S(1)} %get-tuple-element.50.refs_1_), channel_id=1, source_target_pairs={{2,0},{0,2},{3,1},{1,3},{6,4},{4,6},{7,5},{5,7},{10,8},{8,10},{11,... | collective-permute-start | bytes 2359304 | tf_op jit(solution)/shard_map/ppermute | solution.py:299
  26.5 1.8 %collective-permute-start.5 = (bf16[4,4,2,128,128]{4,3,2,1,0:T(8,128)(2,1)S(1)}, bf16[4,4,2,128,128]{4,3,2,1,0:T(8,128)(2,1)S(1)}, u32[]{:S(2)}, u32[]{:S(2)}) collective-permute-start(bf16[4,4,2,128,128]{4,3,2,1,0:T(8,128)(2,1)S(1)} %bitcast.15), channel_id=1, source_target_pairs={{1,0},{0,1},{3,2},{2,3},{5,4},{4,5},{7,6},{6,7},{9,8},{8,9},{11,10... | collective-permute-start | bytes 3145736 | tf_op jit(solution)/shard_map/ppermute | solution.py:299
  28.3 0.6 shard_map.81
  28.9 19.2 %all_to_all.10.chunks = bf16[32,8,128]{2,1,0:T(8,128)(2,1)S(1)} all-to-all(bf16[32,8,128]{2,1,0:T(8,128)(2,1)S(1)} %bitcast.18), channel_id=1, replica_groups=mesh['y'=4,'z'=8,'xh'=2,'xl'=2,'c'=2] {'y','z'}, dimensions={0} | all-to-all | bytes 131072 | tf_op jit(solution)/shard_map/all_to_all | solution.py:368
  48.1 0.5 shard_map.82.mine
  48.7 1.5 %collective-permute-start.7 = (bf16[3,4,2,128,128]{4,3,2,1,0:T(8,128)(2,1)S(1)}, bf16[3,4,2,128,128]{4,3,2,1,0:T(8,128)(2,1)S(1)}, u32[]{:S(2)}, u32[]{:S(2)}) collective-permute-start(bf16[3,4,2,128,128]{4,3,2,1,0:T(8,128)(2,1)S(1)} %collective-permute-done.4.refs_3_), channel_id=1, source_target_pairs={{1,0},{0,1},{3,2},{2,3},{5,4},{4,5},{7,6},{6,7},{9,8},{8,9},{11,10... | collective-permute-start | bytes 2359304 | tf_op jit(solution)/shard_map/ppermute | solution.py:299
  50.2 0.1 collective-permute-start.6
  50.3 2.5 %collective-permute-start.8 = (bf16[4,8,128]{2,1,0:T(8,128)(2,1)S(1)}, bf16[4,8,128]{2,1,0:T(8,128)(2,1)S(1)}, u32[]{:S(2)}, u32[]{:S(2)}) collective-permute-start(bf16[4,8,128]{2,1,0:T(8,128)(2,1)S(1)} %shard_map.82.mine), channel_id=1, source_target_pairs={{4,0},{0,4},{5,1},{1,5},{6,2},{2,6},{7,3},{3,7},{12,8},{8,12},{13,... | collective-permute-start | bytes 24584 | tf_op jit(solution)/shard_map/ppermute | solution.py:299
  52.8 0.9 %collective-permute-start.11 = (bf16[2,32,128]{2,1,0:T(8,128)(2,1)S(1)}, bf16[2,32,128]{2,1,0:T(8,128)(2,1)S(1)}, u32[]{:S(2)}, u32[]{:S(2)}) collective-permute-start(bf16[2,32,128]{2,1,0:T(8,128)(2,1)S(1)} %get-tuple-element.61), channel_id=1, source_target_pairs={{1,0},{2,1},{3,2},{0,3},{5,4},{6,5},{7,6},{4,7},{9,8},{10,9},{11,1... | collective-permute-start | bytes 49160 | tf_op jit(solution)/shard_map/ppermute | solution.py:299
  53.7 2.1 %shard_map.83.whole = f32[4,2,128,128]{3,2,1,0:T(8,128)S(1)} custom-call(bf16[2,128,128]{2,1,0:T(8,128)(2,1)S(1)} %get-tuple-element.55.phi, bf16[4,4,2,128,128]{4,3,2,1,0:T(8,128)(2,1)S(1)} %collective-permute-done.5.whole, bf16[1,4,2,128,128]{4,3,2,1,0:T(8,128)(2,1)S(1)} %copy-done.3, bf16[3,4,2,128,128]{4,3,2,1,0:T(8,128)(2,1)S(1)} %get-tuple-element.50.refs_1_, ...), custom_call_target="tpu_custom_call" | custom-call | flops 1500000000 | bytes 4000000 | tf_op jit(solution)/shard_map/pallas_call | solution.py:286
  55.8 1.5 %collective-permute-start.9 = (bf16[2,32,128]{2,1,0:T(8,128)(2,1)S(1)}, bf16[2,32,128]{2,1,0:T(8,128)(2,1)S(1)}, u32[]{:S(2)}, u32[]{:S(2)}) collective-permute-start(bf16[2,32,128]{2,1,0:T(8,128)(2,1)S(1)} %get-tuple-element.59), channel_id=1, source_target_pairs={{3,0},{0,1},{1,2},{2,3},{7,4},{4,5},{5,6},{6,7},{11,8},{8,9},{9,10... | collective-permute-start | bytes 49160 | tf_op jit(solution)/shard_map/ppermute | solution.py:299
  57.3 0.8 shard_map.84.looped
  58.1 0.6 shard_map.85
  58.7 15.4 %all_to_all.11.spread = bf16[32,4,8,128]{3,2,1,0:T(8,128)(2,1)S(1)} all-to-all(bf16[32,4,8,128]{3,2,1,0:T(8,128)(2,1)S(1)} %shard_map.85), channel_id=1, replica_groups=mesh['y'=4,'z'=8,'xh'=2,'xl'=2,'c'=2] {'y','z'}, dimensions={0} | all-to-all | bytes 524288 | tf_op jit(solution)/shard_map/all_to_all | solution.py:401
  74.1 1.3 %shard_map.86 = (bf16[4,2,32,128]{3,2,1,0:T(8,128)(2,1)}, f32[8,128]{1,0:T(8,128)S(1)}) custom-call(s32[13]{0:T(128)S(1)} %concatenate.3.ints, f32[4,2,128,128]{3,2,1,0:T(8,128)S(1)} %shard_map.84.looped, bf16[32,4,8,128]{3,2,1,0:T(8,128)(2,1)S(1)} %all_to_all.11.spread, bf16[2,32,128]{2,1,0:T(8,128)(2,1)S(1)} %get-tuple-element.64.row0, ...), custom_call_target="tpu_custom_call" | custom-call | flops 100000 | bytes 1000000 | tf_op jit(solution)/shard_map/pallas_call | solution.py:286
  75.4 4.3 %collective-permute-start.12 = (f32[8,128]{1,0:T(8,128)S(1)}, f32[8,128]{1,0:T(8,128)S(1)}, u32[]{:S(2)}, u32[]{:S(2)}) collective-permute-start(f32[8,128]{1,0:T(8,128)S(1)} %get-tuple-element.69.pair0), channel_id=1, source_target_pairs={{3,0},{0,1},{1,2},{2,3},{7,4},{4,5},{5,6},{6,7},{11,8},{8,9},{9,10... | collective-permute-start | bytes 12296 | tf_op jit(solution)/shard_map/ppermute | solution.py:299
  79.7 0.7 collective-permute-start.13
  80.5 1.9 %collective-permute-done.13.pair2 = f32[8,128]{1,0:T(8,128)S(1)} collective-permute-done((f32[8,128]{1,0:T(8,128)S(1)}, f32[8,128]{1,0:T(8,128)S(1)}, u32[]{:S(2)}, u32[]{:S(2)}) %collective-permute-start.13) | collective-permute-done | bytes 4128 | tf_op jit(solution)/shard_map/ppermute | solution.py:299
  82.3 1.1 %collective-permute-done.14.pair3 = f32[8,128]{1,0:T(8,128)S(1)} collective-permute-done((f32[8,128]{1,0:T(8,128)S(1)}, f32[8,128]{1,0:T(8,128)S(1)}, u32[]{:S(2)}, u32[]{:S(2)}) %collective-permute-start.14) | collective-permute-done | bytes 4128 | tf_op jit(solution)/shard_map/ppermute | solution.py:299
  83.5 0.5 shard_map.87
  84.0 0.7 copy.8
  (29 shorter events, 0.2 us)
Async XLA Ops:
  0.6 5.8 %copy-start.1 = (bf16[1,2,3,4,256,128]{5,4,3,2,1,0:T(8,128)(2,1)S(1)}, bf16[1,2,3,4,256,128]{5,4,3,2,1,0:T(8,128)(2,1)}, u32[]{:S(2)}) copy-start(bf16[1,2,3,4,256,128]{5,4,3,2,1,0:T(8,128)(2,1)} %param.6) | copy-start | bytes 4718596
  0.6 5.5 %copy-start.5 = (s32[2,3]{1,0:T(2,128)S(1)}, s32[2,3]{1,0:T(2,128)}, u32[]{:S(2)}) copy-start(s32[2,3]{1,0:T(2,128)} %param.9) | copy-start | bytes 76
  0.7 5.6 %copy-start.6 = (s32[2,2]{1,0:T(2,128)S(1)}, s32[2,2]{1,0:T(2,128)}, u32[]{:S(2)}) copy-start(s32[2,2]{1,0:T(2,128)} %param.10) | copy-start | bytes 52
  0.7 5.8 %copy-start.4 = (bf16[1,3,3,3,2,4,256]{6,5,4,3,2,1,0:T(4,128)(2,1)S(1)}, bf16[1,3,3,3,2,4,256]{6,5,4,3,2,1,0:T(4,128)(2,1)}, u32[]{:S(2)}) copy-start(bf16[1,3,3,3,2,4,256]{6,5,4,3,2,1,0:T(4,128)(2,1)} %param.7) | copy-start | bytes 331780
  2.8 14.3 %collective-permute-start = (bf16[2,3,256,128]{3,2,1,0:T(8,128)(2,1)}, bf16[2,3,256,128]{3,2,1,0:T(8,128)(2,1)S(1)}, u32[]{:S(2)}, u32[]{:S(2)}) collective-permute-start(bf16[2,3,256,128]{3,2,1,0:T(8,128)(2,1)} %get-tuple-element.36), channel_id=1, source_target_pairs={{1,0},{2,1},{3,2},{0,3},{5,4},{6,5},{7,6},{4,7},{9,8},{10,9},{11,1... | collective-permute-start | bytes 1179656 | tf_op jit(solution)/shard_map/ppermute | solution.py:299
  6.2 11.0 %collective-permute-start.1 = (bf16[1,4,2,128,128]{4,3,2,1,0:T(8,128)(2,1)}, bf16[1,4,2,128,128]{4,3,2,1,0:T(8,128)(2,1)S(1)}, u32[]{:S(2)}, u32[]{:S(2)}) collective-permute-start(bf16[1,4,2,128,128]{4,3,2,1,0:T(8,128)(2,1)} %get-tuple-element.38.refs_0_), channel_id=1, source_target_pairs={{2,0},{0,2},{3,1},{1,3},{6,4},{4,6},{7,5},{5,7},{10,8},{8,10},{11,... | collective-permute-start | bytes 786440 | tf_op jit(solution)/shard_map/ppermute | solution.py:299
  6.4 10.8 %copy-start = (bf16[1,4,1,4,2,128,128]{6,5,4,3,2,1,0:T(8,128)(2,1)S(1)}, bf16[1,4,1,4,2,128,128]{6,5,4,3,2,1,0:T(8,128)(2,1)}, u32[]{:S(2)}) copy-start(bf16[1,4,1,4,2,128,128]{6,5,4,3,2,1,0:T(8,128)(2,1)} %param.8) | copy-start | bytes 3145732
  17.2 30.9 %copy-start.2 = (s32[4]{0:T(128)S(1)}, s32[4]{0:T(128)}, u32[]{:S(2)}) copy-start(s32[4]{0:T(128)} %sources.3) | copy-start | bytes 52
  17.2 36.4 %copy-start.3 = (bf16[1,4,2,128,128]{4,3,2,1,0:T(8,128)(2,1)S(1)}, bf16[1,4,2,128,128]{4,3,2,1,0:T(8,128)(2,1)}, u32[]{:S(2)}) copy-start(bf16[1,4,2,128,128]{4,3,2,1,0:T(8,128)(2,1)} %get-tuple-element.38.refs_0_) | copy-start | bytes 786436
  19.4 1.6 %collective-permute-start.2 = (f32[2,2,128,128]{3,2,1,0:T(8,128)S(1)}, f32[2,2,128,128]{3,2,1,0:T(8,128)S(1)}, u32[]{:S(2)}, u32[]{:S(2)}) collective-permute-start(f32[2,2,128,128]{3,2,1,0:T(8,128)S(1)} %get-tuple-element.43), channel_id=1, source_target_pairs={{1,0},{0,1},{3,2},{2,3},{5,4},{4,5},{7,6},{6,7},{9,8},{8,9},{11,10... | collective-permute-start | bytes 786440 | tf_op jit(solution)/shard_map/ppermute | solution.py:299
  21.6 4.0 %collective-permute-start.3 = (bf16[2,128,128]{2,1,0:T(8,128)(2,1)S(1)}, bf16[2,128,128]{2,1,0:T(8,128)(2,1)S(1)}, u32[]{:S(2)}, u32[]{:S(2)}) collective-permute-start(bf16[2,128,128]{2,1,0:T(8,128)(2,1)S(1)} %get-tuple-element.46), channel_id=1, source_target_pairs={{2,0},{0,2},{3,1},{1,3},{6,4},{4,6},{7,5},{5,7},{10,8},{8,10},{11,... | collective-permute-start | bytes 196616 | tf_op jit(solution)/shard_map/ppermute | solution.py:299
  25.5 23.1 %collective-permute-start.4 = (bf16[3,4,2,128,128]{4,3,2,1,0:T(8,128)(2,1)S(1)}, bf16[3,4,2,128,128]{4,3,2,1,0:T(8,128)(2,1)S(1)}, u32[]{:S(2)}, u32[]{:S(2)}) collective-permute-start(bf16[3,4,2,128,128]{4,3,2,1,0:T(8,128)(2,1)S(1)} %get-tuple-element.50.refs_1_), channel_id=1, source_target_pairs={{2,0},{0,2},{3,1},{1,3},{6,4},{4,6},{7,5},{5,7},{10,8},{8,10},{11,... | collective-permute-start | bytes 2359304 | tf_op jit(solution)/shard_map/ppermute | solution.py:299
  26.5 26.3 %collective-permute-start.5 = (bf16[4,4,2,128,128]{4,3,2,1,0:T(8,128)(2,1)S(1)}, bf16[4,4,2,128,128]{4,3,2,1,0:T(8,128)(2,1)S(1)}, u32[]{:S(2)}, u32[]{:S(2)}) collective-permute-start(bf16[4,4,2,128,128]{4,3,2,1,0:T(8,128)(2,1)S(1)} %bitcast.15), channel_id=1, source_target_pairs={{1,0},{0,1},{3,2},{2,3},{5,4},{4,5},{7,6},{6,7},{9,8},{8,9},{11,10... | collective-permute-start | bytes 3145736 | tf_op jit(solution)/shard_map/ppermute | solution.py:299
  48.7 8.6 %collective-permute-start.7 = (bf16[3,4,2,128,128]{4,3,2,1,0:T(8,128)(2,1)S(1)}, bf16[3,4,2,128,128]{4,3,2,1,0:T(8,128)(2,1)S(1)}, u32[]{:S(2)}, u32[]{:S(2)}) collective-permute-start(bf16[3,4,2,128,128]{4,3,2,1,0:T(8,128)(2,1)S(1)} %collective-permute-done.4.refs_3_), channel_id=1, source_target_pairs={{1,0},{0,1},{3,2},{2,3},{5,4},{4,5},{7,6},{6,7},{9,8},{8,9},{11,10... | collective-permute-start | bytes 2359304 | tf_op jit(solution)/shard_map/ppermute | solution.py:299
  50.2 5.6 %collective-permute-start.6 = (bf16[1,4,2,128,128]{4,3,2,1,0:T(8,128)(2,1)S(1)}, bf16[1,4,2,128,128]{4,3,2,1,0:T(8,128)(2,1)S(1)}, u32[]{:S(2)}, u32[]{:S(2)}) collective-permute-start(bf16[1,4,2,128,128]{4,3,2,1,0:T(8,128)(2,1)S(1)} %collective-permute-done.1.refs_2_), channel_id=1, source_target_pairs={{1,0},{0,1},{3,2},{2,3},{5,4},{4,5},{7,6},{6,7},{9,8},{8,9},{11,10... | collective-permute-start | bytes 786440 | tf_op jit(solution)/shard_map/ppermute | solution.py:299
  50.3 7.8 %collective-permute-start.8 = (bf16[4,8,128]{2,1,0:T(8,128)(2,1)S(1)}, bf16[4,8,128]{2,1,0:T(8,128)(2,1)S(1)}, u32[]{:S(2)}, u32[]{:S(2)}) collective-permute-start(bf16[4,8,128]{2,1,0:T(8,128)(2,1)S(1)} %shard_map.82.mine), channel_id=1, source_target_pairs={{4,0},{0,4},{5,1},{1,5},{6,2},{2,6},{7,3},{3,7},{12,8},{8,12},{13,... | collective-permute-start | bytes 24584 | tf_op jit(solution)/shard_map/ppermute | solution.py:299
  52.7 5.4 %collective-permute-start.10 = (bf16[2,32,128]{2,1,0:T(8,128)(2,1)S(1)}, bf16[2,32,128]{2,1,0:T(8,128)(2,1)S(1)}, u32[]{:S(2)}, u32[]{:S(2)}) collective-permute-start(bf16[2,32,128]{2,1,0:T(8,128)(2,1)S(1)} %get-tuple-element.60), channel_id=1, source_target_pairs={{2,0},{3,1},{0,2},{1,3},{6,4},{7,5},{4,6},{5,7},{10,8},{11,9},{8,1... | collective-permute-start | bytes 49160 | tf_op jit(solution)/shard_map/ppermute | solution.py:299
  52.8 5.4 %collective-permute-start.11 = (bf16[2,32,128]{2,1,0:T(8,128)(2,1)S(1)}, bf16[2,32,128]{2,1,0:T(8,128)(2,1)S(1)}, u32[]{:S(2)}, u32[]{:S(2)}) collective-permute-start(bf16[2,32,128]{2,1,0:T(8,128)(2,1)S(1)} %get-tuple-element.61), channel_id=1, source_target_pairs={{1,0},{2,1},{3,2},{0,3},{5,4},{6,5},{7,6},{4,7},{9,8},{10,9},{11,1... | collective-permute-start | bytes 49160 | tf_op jit(solution)/shard_map/ppermute | solution.py:299
  55.8 2.4 %collective-permute-start.9 = (bf16[2,32,128]{2,1,0:T(8,128)(2,1)S(1)}, bf16[2,32,128]{2,1,0:T(8,128)(2,1)S(1)}, u32[]{:S(2)}, u32[]{:S(2)}) collective-permute-start(bf16[2,32,128]{2,1,0:T(8,128)(2,1)S(1)} %get-tuple-element.59), channel_id=1, source_target_pairs={{3,0},{0,1},{1,2},{2,3},{7,4},{4,5},{5,6},{6,7},{11,8},{8,9},{9,10... | collective-permute-start | bytes 49160 | tf_op jit(solution)/shard_map/ppermute | solution.py:299
  75.4 5.1 %collective-permute-start.12 = (f32[8,128]{1,0:T(8,128)S(1)}, f32[8,128]{1,0:T(8,128)S(1)}, u32[]{:S(2)}, u32[]{:S(2)}) collective-permute-start(f32[8,128]{1,0:T(8,128)S(1)} %get-tuple-element.69.pair0), channel_id=1, source_target_pairs={{3,0},{0,1},{1,2},{2,3},{7,4},{4,5},{5,6},{6,7},{11,8},{8,9},{9,10... | collective-permute-start | bytes 12296 | tf_op jit(solution)/shard_map/ppermute | solution.py:299
  79.7 2.6 %collective-permute-start.13 = (f32[8,128]{1,0:T(8,128)S(1)}, f32[8,128]{1,0:T(8,128)S(1)}, u32[]{:S(2)}, u32[]{:S(2)}) collective-permute-start(f32[8,128]{1,0:T(8,128)S(1)} %get-tuple-element.69.pair0), channel_id=1, source_target_pairs={{2,0},{3,1},{0,2},{1,3},{6,4},{7,5},{4,6},{5,7},{10,8},{11,9},{8,1... | collective-permute-start | bytes 12296 | tf_op jit(solution)/shard_map/ppermute | solution.py:299
  80.4 3.0 %collective-permute-start.14 = (f32[8,128]{1,0:T(8,128)S(1)}, f32[8,128]{1,0:T(8,128)S(1)}, u32[]{:S(2)}, u32[]{:S(2)}) collective-permute-start(f32[8,128]{1,0:T(8,128)S(1)} %get-tuple-element.69.pair0), channel_id=1, source_target_pairs={{1,0},{2,1},{3,2},{0,3},{5,4},{6,5},{7,6},{4,7},{9,8},{10,9},{11,1... | collective-permute-start | bytes 12296 | tf_op jit(solution)/shard_map/ppermute | solution.py:299

commit v3 on v2

--- a/solution.py
+++ b/solution.py
@@ -151,7 +151,7 @@
     unit = unit_matrix(128)
     for comp in range(6):
         vt[comp] = dot_nt(unit, halo[comp // 3, comp % 3])
-    transport(links, 0, 2, lambda comp, at, lanes: vt[comp, at, lanes], field)
+    transport(links, links.shape[0] - 1, 2, lambda comp, at, lanes: vt[comp, at, lanes], field)
     rest[...] = tau[1:4]
     core = ints[11] & 1
     edge = dot_nt(phased[...].reshape(1024, 768), field[...])
@@ -194,12 +194,28 @@
         copy.wait()
 
 
-def table_kernel(ints, pair0, pair1, pair2, pair3, table):
-    lane = lax.broadcasted_iota(jnp.int32, (8, 128), 1)
-    total = jnp.zeros((8, 128), F32)
-    for d, got in enumerate((pair0, pair1, pair2, pair3)):
-        total = jnp.where(lane == ((ints[11] + 4 - d) & 3), got[...], total)
-    table[...] = total
+def final_kernel(ints, pair, phi, got1, got2, got3, rows, correlator):
+    own = ints[11]
+    mine = pl.ds(pl.multiple_of(own * 32, 32), 32)
+    for part in range(2):
+        rows[own, part] = phi[part, mine, :]
+    sums = [jnp.sum(pair[...], axis=1, keepdims=True)]
+    for d, got in enumerate((got1, got2, got3), 1):
+        rows[(own + 4 - d) & 3] = got[8:72].astype(BF).reshape(2, 32, 128)
+        sums.append(jnp.sum(got[0:8], axis=1, keepdims=True))
+    sub = lax.broadcasted_iota(jnp.int32, (2, NSRC), 0)
+    lane = lax.broadcasted_iota(jnp.int32, (2, NSRC), 1)
+    for m in range(2):
+        for k in range(2):
+            total = jnp.zeros((8, 1), F32)
+            for d, value in enumerate(sums):
+                total = jnp.where(((own + 4 - d) & 3) == 2 * m + k, value, total)
+            block = jnp.zeros((2, NSRC), F32)
+            for s in range(NSRC):
+                for part in range(2):
+                    value = jnp.broadcast_to(total[2 * s + part : 2 * s + part + 1], (2, NSRC))
+                    block = jnp.where((sub == part) & (lane == s), value, block)
+            correlator[m, k] = block
 
 
 def half_kernel(ints, keep, got, mine, other):
@@ -208,12 +224,9 @@
     other[...] = (keep[1 - chip] + got[1 - chip]).astype(BF)
 
 
-def phi_kernel(ints, mine, got, phi, row0, row1, row2, row3):
-    phi[...] = ((mine[...] + got[...].astype(F32)) * (1.0 / math.sqrt(12.0 * LX * LY * 16))).astype(BF)
-    for d, out in enumerate((row0, row1, row2, row3)):
-        rows = pl.ds(pl.multiple_of(((ints[11] + d) & 3) * 32, 32), 32)
-        for part in range(2):
-            out[part] = phi[part, rows, :]
+def phi_kernel(mine, got, phi):
+    total = mine[...] + got[...].astype(F32)
+    phi[...] = (total * (1.0 / math.sqrt(12.0 * LX * LY * 16))).astype(BF)
 
 
 def pick_kernel(sources, chunks, out):
@@ -265,17 +278,20 @@
         out[s, 1] = total[:, 128:]
 
 
-def close_kernel(ints, looped, spread, row0, row1, row2, row3, rows, pair):
-    for d, got in enumerate((row0, row1, row2, row3)):
-        rows[(ints[11] + 4 - d) & 3] = got[...]
+def close_kernel(ints, looped, spread, phi, pair, send1, send2, send3):
     for s in range(NSRC):
         src_re = spread[0:16, s].astype(F32).reshape(128, 128)
         src_im = spread[16:32, s].astype(F32).reshape(128, 128)
         yr, yi = looped[s, 0], looped[s, 1]
-        re = jnp.sum(yr * src_re + yi * src_im) * (1.0 / (8.0 * 128))
-        im = jnp.sum(yi * src_re - yr * src_im) * (1.0 / (8.0 * 128))
-        pair[2 * s : 2 * s + 1, :] = jnp.full((1, 128), re, F32)
-        pair[2 * s + 1 : 2 * s + 2, :] = jnp.full((1, 128), im, F32)
+        re = jnp.sum(yr * src_re + yi * src_im, axis=0, keepdims=True)
+        im = jnp.sum(yi * src_re - yr * src_im, axis=0, keepdims=True)
+        pair[2 * s : 2 * s + 1, :] = re * (1.0 / (8.0 * 128))
+        pair[2 * s + 1 : 2 * s + 2, :] = im * (1.0 / (8.0 * 128))
+    for d, send in enumerate((send1, send2, send3), 1):
+        send[0:8] = pair[...]
+        rows = pl.ds(pl.multiple_of(((ints[11] + d) & 3) * 32, 32), 32)
+        for part in range(2):
+            send[8 + 32 * part : 40 + 32 * part] = phi[part, rows, :].astype(F32)
 
 
 VMEM = pl.BlockSpec(memory_space=pltpu.VMEM)
@@ -309,6 +325,7 @@
     own = lax.axis_index("xl") * 2 + lax.axis_index("c")
     tau = peramb[0, :, 0]
     piece = [shaped(n, *tau.shape[1:], dtype=BF) for n in (1, 3)]
+    links = gauge_links[0].reshape(54, depth, LX * LY)
     lowest, head = pl.pallas_call(
         pieces_kernel,
         out_shape=(shaped(2, 3, 256, 128, dtype=BF), piece[0]),
@@ -319,7 +336,6 @@
     halo = partner(lowest, GZ)
     near = partner(tau, "c")
     far = [partner(head, "xl")]
-    links = gauge_links[0].reshape(54, depth, LX * LY)
     ints = jnp.concatenate(
         [
             momenta.reshape(6),
@@ -355,23 +371,14 @@
     arrived = partner(other, "xl")
     last, arrived = lax.optimization_barrier((rest, arrived))
     far.append(partner(last, "xl"))
-    block = shaped(2, 32, 128, dtype=BF)
-    phi, *rows = call(
-        phi_kernel,
-        (shaped(2, 128, 128, dtype=BF), block, block, block, block),
-        (ints, mine, arrived),
-        [],
-        10**5,
-        10**6,
-    )
+    phi = call(phi_kernel, shaped(2, 128, 128, dtype=BF), (mine, arrived), [], 10**5, 10**6)
 
     chunks = lax.all_to_all(phi.reshape(32, 8, 128), YZ, 0, 0, tiled=True)
     four = shaped(NSRC, 8, 128, dtype=BF)
     picked = call(pick_kernel, four, (sources, chunks), [], 10**4, 10**5)
     crossed = partner(picked, "xh")
-    phi, _, far, rows = lax.optimization_barrier((phi, picked, far, rows))
+    phi, _, far = lax.optimization_barrier((phi, picked, far))
     diagonal = [partner(piece, "c") for piece in far]
-    rows = rows[:1] + [partner(row, GZ, -d) for d, row in enumerate(rows) if d]
     looped = shaped(NSRC, 2, 128, 128)
     partly = call(
         functools.partial(loop_kernel, start=True),
@@ -389,7 +396,7 @@
         5 * 10**8,
         2 * 10**6,
     )
-    looped, crossed, *rows = lax.optimization_barrier((looped, crossed, *rows))
+    looped, crossed = lax.optimization_barrier((looped, crossed))
     spread = call(
         spread_kernel,
         shaped(32, NSRC, 8, 128, dtype=BF),
@@ -399,18 +406,24 @@
         10**5,
     )
     spread = lax.all_to_all(spread, YZ, 0, 0, tiled=True)
-    rows, pair = call(
+    pair, *sends = call(
         close_kernel,
-        (shaped(4, 2, 32, 128, dtype=BF), shaped(8, 128)),
-        (ints, looped, spread, *rows),
+        (shaped(8, 128), *[shaped(72, 128)] * 3),
+        (ints, looped, spread, phi),
         [],
         10**5,
         10**6,
     )
-    pairs = [pair] + [partner(pair, GZ, -d) for d in range(1, 4)]
-    table = call(table_kernel, shaped(8, 128), (ints, *pairs), [], 10**3, 10**4)
-    correlator = jnp.swapaxes(table[:, :4].reshape(NSRC, 2, 4), 1, 2)
-    return rows.reshape(1, 2, 2, 2, 32, 128), correlator.reshape(NSRC, 1, 2, 2, 2)
+    rows, correlator = call(
+        final_kernel,
+        (shaped(4, 2, 32, 128, dtype=BF), shaped(2, 2, 2, NSRC)),
+        (ints, pair, phi, *[partner(send, GZ, -d) for d, send in enumerate(sends, 1)]),
+        [],
+        10**5,
+        10**6,
+    )
+    correlator = jnp.transpose(correlator, (3, 0, 1, 2))[:, None]
+    return rows.reshape(1, 2, 2, 2, 32, 128), correlator
 
 
 def solution(mesh):

time: 84.9 us -> 81.5 us (0.960)
  starting transfers between devices: 19.7 us -> 17.7 us
    ppermute x15 -> x12, starting transfers between devices: 19.7 us -> 17.7 us  [partner(): lax.ppermute(value, axis, [((i + distance) % n, i) for i in range(n)])]
    ppermute x15 -> x12, waiting for transfers between devices: 6.47 us -> 5.86 us  [partner(): lax.ppermute(value, axis, [((i + distance) % n, i) for i in range(n)])]
  transfers between devices with their start and end apart: 15 -> 12, of which waited for: 4 -> 3; matrix products, arithmetic and copies ran while one was open for 0% -> 0% of each run, Pallas kernels for 17% -> 18%
where the time goes in v3:
time: 81.5 us; the launch traced here: 81.3 us
  blocking collectives  35.1 us (43%)
  Pallas kernels  21.6 us (27%)
  starting transfers between devices  17.7 us (22%)
  waiting for transfers between devices  5.86 us (7%)
  between operations  0.82 us (1%)
    pallas_call x10, Pallas kernels, call(): pl.pallas_call(kernel, out_shape=outs, in_specs=[SMEM if x.ndim == 1 else...  19.4 us
    all_to_all x1, blocking collectives, on_device(): chunks = lax.all_to_all(phi.reshape(32, 8, 128), YZ, 0, 0, tiled=True)  19.2 us
    ppermute x12, starting transfers between devices, partner(): lax.ppermute(value, axis, [((i + distance) % n, i) for i in range(n)])  17.7 us
    all_to_all x1, blocking collectives, on_device(): spread = lax.all_to_all(spread, YZ, 0, 0, tiled=True)  15.8 us
    ppermute x12, waiting for transfers between devices, partner(): lax.ppermute(value, axis, [((i + distance) % n, i) for i in range(n)])  5.86 us
    pallas_call x1, Pallas kernels, on_device(): pl.pallas_call(pieces_kernel, out_shape=(shaped(2, 3, 256, 128, dtype=BF)...  2.18 us
  transfers between devices with their start and end apart: 12, of which 3 were waited for; matrix products, arithmetic and copies ran while one was open for 0% of the time, Pallas kernels for 18%

profile of v3, /device:TPU:1, one launch (start us, length us, event | category | flops | bytes accessed | tf_op | source)
XLA Modules:
  0.0 81.3 jit_solution(12501983334553603617)
XLA Ops:
  0.7 2.2 %shard_map.77 = (bf16[2,3,256,128]{3,2,1,0:T(8,128)(2,1)}, bf16[1,4,2,128,128]{4,3,2,1,0:T(8,128)(2,1)}) custom-call(bf16[2,3,4,256,128]{4,3,2,1,0:T(8,128)(2,1)} %bitcast.15, bf16[4,4,2,128,128]{4,3,2,1,0:T(8,128)(2,1)} %bitcast.11), custom_call_target="tpu_custom_call" | custom-call | tf_op jit(solution)/shard_map/pallas_call | solution.py:329
  2.9 3.3 %collective-permute-start = (bf16[2,3,256,128]{3,2,1,0:T(8,128)(2,1)}, bf16[2,3,256,128]{3,2,1,0:T(8,128)(2,1)S(1)}, u32[]{:S(2)}, u32[]{:S(2)}) collective-permute-start(bf16[2,3,256,128]{3,2,1,0:T(8,128)(2,1)} %get-tuple-element.27), channel_id=1, source_target_pairs={{1,0},{2,1},{3,2},{0,3},{5,4},{6,5},{7,6},{4,7},{9,8},{10,9},{11,1... | collective-permute-start | bytes 1179656 | tf_op jit(solution)/shard_map/ppermute | solution.py:315
  6.2 0.0 collective-permute-start.1
  6.2 0.1 reshape.16
  6.3 0.1 reshape.17
  6.3 0.1 concatenate.3.ints
  6.4 10.7 %shard_map.78 = (f32[4,512,256]{2,1,0:T(8,128)S(1)}, bf16[2,512,768]{2,1,0:T(8,128)(2,1)S(1)}, f32[1,54,256]{2,1,0:T(8,128)S(1)}) custom-call(s32[13]{0:T(128)S(1)} %concatenate.3.ints, bf16[2,3,4,256,128]{4,3,2,1,0:T(8,128)(2,1)S(1)} %bitcast.16, bf16[54,4,256]{2,1,0:T(4,128)(2,1)S(1)} %bitcast.17), custom_call_target="tpu_custom_call" | custom-call | flops 4000000000 | bytes 5000000 | tf_op jit(solution)/shard_map/pallas_call | solution.py:302
  17.2 0.0 copy-start.2
  17.2 2.1 %shard_map.79 = (f32[2,2,128,128]{3,2,1,0:T(8,128)S(1)}, f32[2,2,128,128]{3,2,1,0:T(8,128)S(1)}, bf16[3,4,2,128,128]{4,3,2,1,0:T(8,128)(2,1)S(1)}) custom-call(s32[13]{0:T(128)S(1)} %concatenate.3.ints, bf16[2,3,256,128]{3,2,1,0:T(8,128)(2,1)S(1)} %collective-permute-done.halo, f32[1,54,256]{2,1,0:T(8,128)S(1)} %get-tuple-element.28.links, ...), custom_call_target="tpu_custom_call" | custom-call | flops 500000000 | bytes 5000000 | tf_op jit(solution)/shard_map/pallas_call | solution.py:302
  19.4 0.4 collective-permute-start.2
  19.7 1.3 %collective-permute-done.2.got = f32[2,2,128,128]{3,2,1,0:T(8,128)S(1)} collective-permute-done((f32[2,2,128,128]{3,2,1,0:T(8,128)S(1)}, f32[2,2,128,128]{3,2,1,0:T(8,128)S(1)}, u32[]{:S(2)}, u32[]{:S(2)}) %collective-permute-start.2) | collective-permute-done | bytes 262176 | tf_op jit(solution)/shard_map/ppermute | solution.py:315
  21.0 0.6 shard_map.80
  21.6 1.8 %collective-permute-start.3 = (bf16[2,128,128]{2,1,0:T(8,128)(2,1)S(1)}, bf16[2,128,128]{2,1,0:T(8,128)(2,1)S(1)}, u32[]{:S(2)}, u32[]{:S(2)}) collective-permute-start(bf16[2,128,128]{2,1,0:T(8,128)(2,1)S(1)} %get-tuple-element.37), channel_id=1, source_target_pairs={{2,0},{0,2},{3,1},{1,3},{6,4},{4,6},{7,5},{5,7},{10,8},{8,10},{11,... | collective-permute-start | bytes 196616 | tf_op jit(solution)/shard_map/ppermute | solution.py:315
  23.4 2.2 %collective-permute-done.3.got = bf16[2,128,128]{2,1,0:T(8,128)(2,1)S(1)} collective-permute-done((bf16[2,128,128]{2,1,0:T(8,128)(2,1)S(1)}, bf16[2,128,128]{2,1,0:T(8,128)(2,1)S(1)}, u32[]{:S(2)}, u32[]{:S(2)}) %collective-permute-start.3) | collective-permute-done | bytes 65568 | tf_op jit(solution)/shard_map/ppermute | solution.py:315
  25.6 1.0 %collective-permute-start.4 = (bf16[3,4,2,128,128]{4,3,2,1,0:T(8,128)(2,1)S(1)}, bf16[3,4,2,128,128]{4,3,2,1,0:T(8,128)(2,1)S(1)}, u32[]{:S(2)}, u32[]{:S(2)}) collective-permute-start(bf16[3,4,2,128,128]{4,3,2,1,0:T(8,128)(2,1)S(1)} %get-tuple-element.40.refs_1_), channel_id=1, source_target_pairs={{2,0},{0,2},{3,1},{1,3},{6,4},{4,6},{7,5},{5,7},{10,8},{8,10},{11,... | collective-permute-start | bytes 2359304 | tf_op jit(solution)/shard_map/ppermute | solution.py:315
  26.5 1.8 %collective-permute-start.5 = (bf16[4,4,2,128,128]{4,3,2,1,0:T(8,128)(2,1)S(1)}, bf16[4,4,2,128,128]{4,3,2,1,0:T(8,128)(2,1)S(1)}, u32[]{:S(2)}, u32[]{:S(2)}) collective-permute-start(bf16[4,4,2,128,128]{4,3,2,1,0:T(8,128)(2,1)S(1)} %bitcast.13), channel_id=1, source_target_pairs={{1,0},{0,1},{3,2},{2,3},{5,4},{4,5},{7,6},{6,7},{9,8},{8,9},{11,10... | collective-permute-start | bytes 3145736 | tf_op jit(solution)/shard_map/ppermute | solution.py:315
  28.3 19.2 %all_to_all.10.chunks = bf16[32,8,128]{2,1,0:T(8,128)(2,1)S(1)} all-to-all(bf16[32,8,128]{2,1,0:T(8,128)(2,1)S(1)} %bitcast.14), channel_id=1, replica_groups=mesh['y'=4,'z'=8,'xh'=2,'xl'=2,'c'=2] {'y','z'}, dimensions={0} | all-to-all | bytes 131072 | tf_op jit(solution)/shard_map/all_to_all | solution.py:376
  47.6 0.5 shard_map.82.mine
  48.2 1.5 %collective-permute-start.7 = (bf16[3,4,2,128,128]{4,3,2,1,0:T(8,128)(2,1)S(1)}, bf16[3,4,2,128,128]{4,3,2,1,0:T(8,128)(2,1)S(1)}, u32[]{:S(2)}, u32[]{:S(2)}) collective-permute-start(bf16[3,4,2,128,128]{4,3,2,1,0:T(8,128)(2,1)S(1)} %collective-permute-done.4.refs_3_), channel_id=1, source_target_pairs={{1,0},{0,1},{3,2},{2,3},{5,4},{4,5},{7,6},{6,7},{9,8},{8,9},{11,10... | collective-permute-start | bytes 2359304 | tf_op jit(solution)/shard_map/ppermute | solution.py:315
  49.7 0.1 collective-permute-start.6
  49.8 2.5 %collective-permute-start.8 = (bf16[4,8,128]{2,1,0:T(8,128)(2,1)S(1)}, bf16[4,8,128]{2,1,0:T(8,128)(2,1)S(1)}, u32[]{:S(2)}, u32[]{:S(2)}) collective-permute-start(bf16[4,8,128]{2,1,0:T(8,128)(2,1)S(1)} %shard_map.82.mine), channel_id=1, source_target_pairs={{4,0},{0,4},{5,1},{1,5},{6,2},{2,6},{7,3},{3,7},{12,8},{8,12},{13,... | collective-permute-start | bytes 24584 | tf_op jit(solution)/shard_map/ppermute | solution.py:315
  52.2 0.0 collective-permute-done.5.whole
  52.2 2.1 %shard_map.83.whole = f32[4,2,128,128]{3,2,1,0:T(8,128)S(1)} custom-call(bf16[2,128,128]{2,1,0:T(8,128)(2,1)S(1)} %shard_map.81.phi, bf16[4,4,2,128,128]{4,3,2,1,0:T(8,128)(2,1)S(1)} %collective-permute-done.5.whole, bf16[1,4,2,128,128]{4,3,2,1,0:T(8,128)(2,1)S(1)} %copy-done.3, bf16[3,4,2,128,128]{4,3,2,1,0:T(8,128)(2,1)S(1)} %get-tuple-element.40.refs_1_, ...), custom_call_target="tpu_custom_call" | custom-call | flops 1500000000 | bytes 4000000 | tf_op jit(solution)/shard_map/pallas_call | solution.py:302
  54.3 0.8 %shard_map.84.looped = f32[4,2,128,128]{3,2,1,0:T(8,128)S(1)} custom-call(bf16[2,128,128]{2,1,0:T(8,128)(2,1)S(1)} %shard_map.81.phi, f32[4,2,128,128]{3,2,1,0:T(8,128)S(1)} %shard_map.83.whole, bf16[1,4,2,128,128]{4,3,2,1,0:T(8,128)(2,1)S(1)} %collective-permute-done.6.refs_0_, bf16[3,4,2,128,128]{4,3,2,1,0:T(8,128)(2,1)S(1)} %collective-permute-done.7.refs_1_), custom_call_target="tpu_custom_call" | custom-call | flops 500000000 | bytes 2000000 | tf_op jit(solution)/shard_map/pallas_call | solution.py:302
  55.2 0.6 shard_map.85
  55.8 15.8 %all_to_all.11.spread = bf16[32,4,8,128]{3,2,1,0:T(8,128)(2,1)S(1)} all-to-all(bf16[32,4,8,128]{3,2,1,0:T(8,128)(2,1)S(1)} %shard_map.85), channel_id=1, replica_groups=mesh['y'=4,'z'=8,'xh'=2,'xl'=2,'c'=2] {'y','z'}, dimensions={0} | all-to-all | bytes 524288 | tf_op jit(solution)/shard_map/all_to_all | solution.py:408
  71.6 0.7 shard_map.86
  72.3 0.4 collective-permute-start.10
  72.7 3.9 %collective-permute-start.11 = (f32[72,128]{1,0:T(8,128)S(1)}, f32[72,128]{1,0:T(8,128)S(1)}, u32[]{:S(2)}, u32[]{:S(2)}) collective-permute-start(f32[72,128]{1,0:T(8,128)S(1)} %get-tuple-element.49), channel_id=1, source_target_pairs={{1,0},{2,1},{3,2},{0,3},{5,4},{6,5},{7,6},{4,7},{9,8},{10,9},{11,1... | collective-permute-start | bytes 110600 | tf_op jit(solution)/shard_map/ppermute | solution.py:315
  76.6 1.0 %collective-permute-start.9 = (f32[72,128]{1,0:T(8,128)S(1)}, f32[72,128]{1,0:T(8,128)S(1)}, u32[]{:S(2)}, u32[]{:S(2)}) collective-permute-start(f32[72,128]{1,0:T(8,128)S(1)} %get-tuple-element.47), channel_id=1, source_target_pairs={{3,0},{0,1},{1,2},{2,3},{7,4},{4,5},{5,6},{6,7},{11,8},{8,9},{9,10... | collective-permute-start | bytes 110600 | tf_op jit(solution)/shard_map/ppermute | solution.py:315
  77.7 2.4 %collective-permute-done.11.got3 = f32[72,128]{1,0:T(8,128)S(1)} collective-permute-done((f32[72,128]{1,0:T(8,128)S(1)}, f32[72,128]{1,0:T(8,128)S(1)}, u32[]{:S(2)}, u32[]{:S(2)}) %collective-permute-start.11) | collective-permute-done | bytes 36896 | tf_op jit(solution)/shard_map/ppermute | solution.py:315
  80.1 1.2 %shard_map.87 = (bf16[4,2,32,128]{3,2,1,0:T(8,128)(2,1)}, f32[2,2,2,4]{3,2,1,0:T(2,128)}) custom-call(s32[13]{0:T(128)S(1)} %concatenate.3.ints, f32[8,128]{1,0:T(8,128)S(1)} %get-tuple-element.46.pair, bf16[2,128,128]{2,1,0:T(8,128)(2,1)S(1)} %shard_map.81.phi, f32[72,128]{1,0:T(8,128)S(1)} %collective-permute-done.9.got1, ...), custom_call_target="tpu_custom_call" | custom-call | flops 100000 | bytes 1000000 | tf_op jit(solution)/shard_map/pallas_call | solution.py:302
  (22 shorter events, 0.1 us)
Async XLA Ops:
  0.6 5.8 %copy-start.1 = (bf16[1,2,3,4,256,128]{5,4,3,2,1,0:T(8,128)(2,1)S(1)}, bf16[1,2,3,4,256,128]{5,4,3,2,1,0:T(8,128)(2,1)}, u32[]{:S(2)}) copy-start(bf16[1,2,3,4,256,128]{5,4,3,2,1,0:T(8,128)(2,1)} %param.6) | copy-start | bytes 4718596
  0.6 5.5 %copy-start.5 = (s32[2,3]{1,0:T(2,128)S(1)}, s32[2,3]{1,0:T(2,128)}, u32[]{:S(2)}) copy-start(s32[2,3]{1,0:T(2,128)} %param.9) | copy-start | bytes 76
  0.7 5.6 %copy-start.6 = (s32[2,2]{1,0:T(2,128)S(1)}, s32[2,2]{1,0:T(2,128)}, u32[]{:S(2)}) copy-start(s32[2,2]{1,0:T(2,128)} %param.10) | copy-start | bytes 52
  0.7 5.8 %copy-start.4 = (bf16[1,3,3,3,2,4,256]{6,5,4,3,2,1,0:T(4,128)(2,1)S(1)}, bf16[1,3,3,3,2,4,256]{6,5,4,3,2,1,0:T(4,128)(2,1)}, u32[]{:S(2)}) copy-start(bf16[1,3,3,3,2,4,256]{6,5,4,3,2,1,0:T(4,128)(2,1)} %param.7) | copy-start | bytes 331780
  2.9 14.3 %collective-permute-start = (bf16[2,3,256,128]{3,2,1,0:T(8,128)(2,1)}, bf16[2,3,256,128]{3,2,1,0:T(8,128)(2,1)S(1)}, u32[]{:S(2)}, u32[]{:S(2)}) collective-permute-start(bf16[2,3,256,128]{3,2,1,0:T(8,128)(2,1)} %get-tuple-element.27), channel_id=1, source_target_pairs={{1,0},{2,1},{3,2},{0,3},{5,4},{6,5},{7,6},{4,7},{9,8},{10,9},{11,1... | collective-permute-start | bytes 1179656 | tf_op jit(solution)/shard_map/ppermute | solution.py:315
  6.2 11.0 %collective-permute-start.1 = (bf16[1,4,2,128,128]{4,3,2,1,0:T(8,128)(2,1)}, bf16[1,4,2,128,128]{4,3,2,1,0:T(8,128)(2,1)S(1)}, u32[]{:S(2)}, u32[]{:S(2)}) collective-permute-start(bf16[1,4,2,128,128]{4,3,2,1,0:T(8,128)(2,1)} %get-tuple-element.29.refs_0_), channel_id=1, source_target_pairs={{2,0},{0,2},{3,1},{1,3},{6,4},{4,6},{7,5},{5,7},{10,8},{8,10},{11,... | collective-permute-start | bytes 786440 | tf_op jit(solution)/shard_map/ppermute | solution.py:315
  6.4 10.8 %copy-start = (bf16[1,4,1,4,2,128,128]{6,5,4,3,2,1,0:T(8,128)(2,1)S(1)}, bf16[1,4,1,4,2,128,128]{6,5,4,3,2,1,0:T(8,128)(2,1)}, u32[]{:S(2)}) copy-start(bf16[1,4,1,4,2,128,128]{6,5,4,3,2,1,0:T(8,128)(2,1)} %param.8) | copy-start | bytes 3145732
  17.2 30.4 %copy-start.2 = (s32[4]{0:T(128)S(1)}, s32[4]{0:T(128)}, u32[]{:S(2)}) copy-start(s32[4]{0:T(128)} %sources.3) | copy-start | bytes 52
  17.2 35.0 %copy-start.3 = (bf16[1,4,2,128,128]{4,3,2,1,0:T(8,128)(2,1)S(1)}, bf16[1,4,2,128,128]{4,3,2,1,0:T(8,128)(2,1)}, u32[]{:S(2)}) copy-start(bf16[1,4,2,128,128]{4,3,2,1,0:T(8,128)(2,1)} %get-tuple-element.29.refs_0_) | copy-start | bytes 786436
  19.4 1.6 %collective-permute-start.2 = (f32[2,2,128,128]{3,2,1,0:T(8,128)S(1)}, f32[2,2,128,128]{3,2,1,0:T(8,128)S(1)}, u32[]{:S(2)}, u32[]{:S(2)}) collective-permute-start(f32[2,2,128,128]{3,2,1,0:T(8,128)S(1)} %get-tuple-element.34), channel_id=1, source_target_pairs={{1,0},{0,1},{3,2},{2,3},{5,4},{4,5},{7,6},{6,7},{9,8},{8,9},{11,10... | collective-permute-start | bytes 786440 | tf_op jit(solution)/shard_map/ppermute | solution.py:315
  21.6 4.0 %collective-permute-start.3 = (bf16[2,128,128]{2,1,0:T(8,128)(2,1)S(1)}, bf16[2,128,128]{2,1,0:T(8,128)(2,1)S(1)}, u32[]{:S(2)}, u32[]{:S(2)}) collective-permute-start(bf16[2,128,128]{2,1,0:T(8,128)(2,1)S(1)} %get-tuple-element.37), channel_id=1, source_target_pairs={{2,0},{0,2},{3,1},{1,3},{6,4},{4,6},{7,5},{5,7},{10,8},{8,10},{11,... | collective-permute-start | bytes 196616 | tf_op jit(solution)/shard_map/ppermute | solution.py:315
  25.6 22.6 %collective-permute-start.4 = (bf16[3,4,2,128,128]{4,3,2,1,0:T(8,128)(2,1)S(1)}, bf16[3,4,2,128,128]{4,3,2,1,0:T(8,128)(2,1)S(1)}, u32[]{:S(2)}, u32[]{:S(2)}) collective-permute-start(bf16[3,4,2,128,128]{4,3,2,1,0:T(8,128)(2,1)S(1)} %get-tuple-element.40.refs_1_), channel_id=1, source_target_pairs={{2,0},{0,2},{3,1},{1,3},{6,4},{4,6},{7,5},{5,7},{10,8},{8,10},{11,... | collective-permute-start | bytes 2359304 | tf_op jit(solution)/shard_map/ppermute | solution.py:315
  26.5 25.7 %collective-permute-start.5 = (bf16[4,4,2,128,128]{4,3,2,1,0:T(8,128)(2,1)S(1)}, bf16[4,4,2,128,128]{4,3,2,1,0:T(8,128)(2,1)S(1)}, u32[]{:S(2)}, u32[]{:S(2)}) collective-permute-start(bf16[4,4,2,128,128]{4,3,2,1,0:T(8,128)(2,1)S(1)} %bitcast.13), channel_id=1, source_target_pairs={{1,0},{0,1},{3,2},{2,3},{5,4},{4,5},{7,6},{6,7},{9,8},{8,9},{11,10... | collective-permute-start | bytes 3145736 | tf_op jit(solution)/shard_map/ppermute | solution.py:315
  48.2 6.2 %collective-permute-start.7 = (bf16[3,4,2,128,128]{4,3,2,1,0:T(8,128)(2,1)S(1)}, bf16[3,4,2,128,128]{4,3,2,1,0:T(8,128)(2,1)S(1)}, u32[]{:S(2)}, u32[]{:S(2)}) collective-permute-start(bf16[3,4,2,128,128]{4,3,2,1,0:T(8,128)(2,1)S(1)} %collective-permute-done.4.refs_3_), channel_id=1, source_target_pairs={{1,0},{0,1},{3,2},{2,3},{5,4},{4,5},{7,6},{6,7},{9,8},{8,9},{11,10... | collective-permute-start | bytes 2359304 | tf_op jit(solution)/shard_map/ppermute | solution.py:315
  49.7 4.7 %collective-permute-start.6 = (bf16[1,4,2,128,128]{4,3,2,1,0:T(8,128)(2,1)S(1)}, bf16[1,4,2,128,128]{4,3,2,1,0:T(8,128)(2,1)S(1)}, u32[]{:S(2)}, u32[]{:S(2)}) collective-permute-start(bf16[1,4,2,128,128]{4,3,2,1,0:T(8,128)(2,1)S(1)} %collective-permute-done.1.refs_2_), channel_id=1, source_target_pairs={{1,0},{0,1},{3,2},{2,3},{5,4},{4,5},{7,6},{6,7},{9,8},{8,9},{11,10... | collective-permute-start | bytes 786440 | tf_op jit(solution)/shard_map/ppermute | solution.py:315
  49.8 5.4 %collective-permute-start.8 = (bf16[4,8,128]{2,1,0:T(8,128)(2,1)S(1)}, bf16[4,8,128]{2,1,0:T(8,128)(2,1)S(1)}, u32[]{:S(2)}, u32[]{:S(2)}) collective-permute-start(bf16[4,8,128]{2,1,0:T(8,128)(2,1)S(1)} %shard_map.82.mine), channel_id=1, source_target_pairs={{4,0},{0,4},{5,1},{1,5},{6,2},{2,6},{7,3},{3,7},{12,8},{8,12},{13,... | collective-permute-start | bytes 24584 | tf_op jit(solution)/shard_map/ppermute | solution.py:315
  72.3 5.4 %collective-permute-start.10 = (f32[72,128]{1,0:T(8,128)S(1)}, f32[72,128]{1,0:T(8,128)S(1)}, u32[]{:S(2)}, u32[]{:S(2)}) collective-permute-start(f32[72,128]{1,0:T(8,128)S(1)} %get-tuple-element.48), channel_id=1, source_target_pairs={{2,0},{3,1},{0,2},{1,3},{6,4},{7,5},{4,6},{5,7},{10,8},{11,9},{8,1... | collective-permute-start | bytes 110600 | tf_op jit(solution)/shard_map/ppermute | solution.py:315
  72.7 7.4 %collective-permute-start.11 = (f32[72,128]{1,0:T(8,128)S(1)}, f32[72,128]{1,0:T(8,128)S(1)}, u32[]{:S(2)}, u32[]{:S(2)}) collective-permute-start(f32[72,128]{1,0:T(8,128)S(1)} %get-tuple-element.49), channel_id=1, source_target_pairs={{1,0},{2,1},{3,2},{0,3},{5,4},{6,5},{7,6},{4,7},{9,8},{10,9},{11,1... | collective-permute-start | bytes 110600 | tf_op jit(solution)/shard_map/ppermute | solution.py:315
  76.6 3.5 %collective-permute-start.9 = (f32[72,128]{1,0:T(8,128)S(1)}, f32[72,128]{1,0:T(8,128)S(1)}, u32[]{:S(2)}, u32[]{:S(2)}) collective-permute-start(f32[72,128]{1,0:T(8,128)S(1)} %get-tuple-element.47), channel_id=1, source_target_pairs={{3,0},{0,1},{1,2},{2,3},{7,4},{4,5},{5,6},{6,7},{11,8},{8,9},{9,10... | collective-permute-start | bytes 110600 | tf_op jit(solution)/shard_map/ppermute | solution.py:315

commit v4 on v3

--- a/solution.py
+++ b/solution.py
@@ -377,25 +377,23 @@
     four = shaped(NSRC, 8, 128, dtype=BF)
     picked = call(pick_kernel, four, (sources, chunks), [], 10**4, 10**5)
     crossed = partner(picked, "xh")
-    phi, _, far = lax.optimization_barrier((phi, picked, far))
-    diagonal = [partner(piece, "c") for piece in far]
-    looped = shaped(NSRC, 2, 128, 128)
-    partly = call(
-        functools.partial(loop_kernel, start=True),
-        looped,
-        (phi, near, head, rest, *far),
-        [],
-        15 * 10**8,
-        4 * 10**6,
-    )
-    looped = call(
-        functools.partial(loop_kernel, start=False),
-        looped,
-        (phi, partly, *diagonal),
-        [],
-        5 * 10**8,
-        2 * 10**6,
-    )
+    phi, _ = lax.optimization_barrier((phi, picked))
+
+    def loop(start, total, *taus):
+        return call(
+            functools.partial(loop_kernel, start=start),
+            shaped(NSRC, 2, 128, 128),
+            (phi, total, *taus),
+            [],
+            5 * 10**8 * (1 + start),
+            2 * 10**6 * (1 + start),
+        )
+
+    looped = loop(True, near, head, rest)
+    looped, far = lax.optimization_barrier((looped, far))
+    diagonal = [partner(one, "c") for one in far]
+    looped = loop(False, looped, *far)
+    looped = loop(False, looped, *diagonal)
     looped, crossed = lax.optimization_barrier((looped, crossed))
     spread = call(
         spread_kernel,

time: 81.5 us -> 81 us (level)
  blocking collectives: 35.1 us -> 31.8 us
  Pallas kernels: 21.6 us -> 23.1 us
  local copies, waits for them, and re-layouts: 0.28 us -> 1.17 us
    all_to_all x1, blocking collectives: 15.8 us -> 13.1 us  [on_device(): spread = lax.all_to_all(spread, YZ, 0, 0, tiled=True)]
    pallas_call x10 -> x11, Pallas kernels: 19.4 us -> 20.9 us  [call(): pl.pallas_call(kernel, out_shape=outs, in_specs=[SMEM if x.ndim == 1 else...]
    unnamed x14, local copies, waits for them, and re-layouts: 0.03 us -> 0.93 us
  transfers between devices with their start and end apart: 12 -> 12, of which waited for: 3 -> 3; matrix products, arithmetic and copies ran while one was open for 0% -> 0% of each run, Pallas kernels for 18% -> 23%
where the time goes in v4:
time: 81 us; the launch traced here: 80.8 us
  blocking collectives  31.8 us (39%)
  Pallas kernels  23.1 us (29%)
  starting transfers between devices  18 us (22%)
  waiting for transfers between devices  5.92 us (7%)
  local copies, waits for them, and re-layouts  1.17 us (1%)
  between operations  0.83 us (1%)
    pallas_call x11, Pallas kernels, call(): pl.pallas_call(kernel, out_shape=outs, in_specs=[SMEM if x.ndim == 1 else...  20.9 us
    all_to_all x1, blocking collectives, on_device(): chunks = lax.all_to_all(phi.reshape(32, 8, 128), YZ, 0, 0, tiled=True)  18.6 us
    ppermute x12, starting transfers between devices, partner(): lax.ppermute(value, axis, [((i + distance) % n, i) for i in range(n)])  18 us
    all_to_all x1, blocking collectives, on_device(): spread = lax.all_to_all(spread, YZ, 0, 0, tiled=True)  13.1 us
    ppermute x12, waiting for transfers between devices, partner(): lax.ppermute(value, axis, [((i + distance) % n, i) for i in range(n)])  5.92 us
    pallas_call x1, Pallas kernels, on_device(): pl.pallas_call(pieces_kernel, out_shape=(shaped(2, 3, 256, 128, dtype=BF)...  2.21 us
  transfers between devices with their start and end apart: 12, of which 3 were waited for; matrix products, arithmetic and copies ran while one was open for 0% of the time, Pallas kernels for 23%

profile of v4, /device:TPU:1, one launch (start us, length us, event | category | flops | bytes accessed | tf_op | source)
XLA Modules:
  0.0 80.8 jit_solution(6101211692411060242)
XLA Ops:
  0.7 2.2 %shard_map.77 = (bf16[2,3,256,128]{3,2,1,0:T(8,128)(2,1)}, bf16[1,4,2,128,128]{4,3,2,1,0:T(8,128)(2,1)}) custom-call(bf16[2,3,4,256,128]{4,3,2,1,0:T(8,128)(2,1)} %bitcast.15, bf16[4,4,2,128,128]{4,3,2,1,0:T(8,128)(2,1)} %bitcast.11), custom_call_target="tpu_custom_call" | custom-call | tf_op jit(solution)/shard_map/pallas_call | solution.py:329
  2.9 3.3 %collective-permute-start = (bf16[2,3,256,128]{3,2,1,0:T(8,128)(2,1)}, bf16[2,3,256,128]{3,2,1,0:T(8,128)(2,1)S(1)}, u32[]{:S(2)}, u32[]{:S(2)}) collective-permute-start(bf16[2,3,256,128]{3,2,1,0:T(8,128)(2,1)} %get-tuple-element.28), channel_id=1, source_target_pairs={{1,0},{2,1},{3,2},{0,3},{5,4},{6,5},{7,6},{4,7},{9,8},{10,9},{11,1... | collective-permute-start | bytes 1179656 | tf_op jit(solution)/shard_map/ppermute | solution.py:315
  6.2 0.1 collective-permute-start.4
  6.3 0.1 reshape.16
  6.4 0.1 reshape.17
  6.5 0.1 concatenate.3.ints
  6.6 0.9 %copy-done.4 = bf16[1,3,3,3,2,4,256]{6,5,4,3,2,1,0:T(4,128)(2,1)S(1)} copy-done((bf16[1,3,3,3,2,4,256]{6,5,4,3,2,1,0:T(4,128)(2,1)S(1)}, bf16[1,3,3,3,2,4,256]{6,5,4,3,2,1,0:T(4,128)(2,1)}, u32[]{:S(2)}) %copy-start.4) | copy-done | bytes 110616
  7.5 10.7 %shard_map.78 = (f32[4,512,256]{2,1,0:T(8,128)S(1)}, bf16[2,512,768]{2,1,0:T(8,128)(2,1)S(1)}, f32[1,54,256]{2,1,0:T(8,128)S(1)}) custom-call(s32[13]{0:T(128)S(1)} %concatenate.3.ints, bf16[2,3,4,256,128]{4,3,2,1,0:T(8,128)(2,1)S(1)} %bitcast.16, bf16[54,4,256]{2,1,0:T(4,128)(2,1)S(1)} %bitcast.17), custom_call_target="tpu_custom_call" | custom-call | flops 4000000000 | bytes 5000000 | tf_op jit(solution)/shard_map/pallas_call | solution.py:302
  18.2 0.0 copy-start.2
  18.3 2.1 %shard_map.79 = (f32[2,2,128,128]{3,2,1,0:T(8,128)S(1)}, f32[2,2,128,128]{3,2,1,0:T(8,128)S(1)}, bf16[3,4,2,128,128]{4,3,2,1,0:T(8,128)(2,1)S(1)}) custom-call(s32[13]{0:T(128)S(1)} %concatenate.3.ints, bf16[2,3,256,128]{3,2,1,0:T(8,128)(2,1)S(1)} %collective-permute-done.halo, f32[1,54,256]{2,1,0:T(8,128)S(1)} %get-tuple-element.29.links, ...), custom_call_target="tpu_custom_call" | custom-call | flops 500000000 | bytes 5000000 | tf_op jit(solution)/shard_map/pallas_call | solution.py:302
  20.4 0.5 collective-permute-start.2
  20.9 1.2 %collective-permute-done.2.got = f32[2,2,128,128]{3,2,1,0:T(8,128)S(1)} collective-permute-done((f32[2,2,128,128]{3,2,1,0:T(8,128)S(1)}, f32[2,2,128,128]{3,2,1,0:T(8,128)S(1)}, u32[]{:S(2)}, u32[]{:S(2)}) %collective-permute-start.2) | collective-permute-done | bytes 262176 | tf_op jit(solution)/shard_map/ppermute | solution.py:315
  22.0 0.6 shard_map.80
  22.6 1.8 %collective-permute-start.3 = (bf16[2,128,128]{2,1,0:T(8,128)(2,1)S(1)}, bf16[2,128,128]{2,1,0:T(8,128)(2,1)S(1)}, u32[]{:S(2)}, u32[]{:S(2)}) collective-permute-start(bf16[2,128,128]{2,1,0:T(8,128)(2,1)S(1)} %get-tuple-element.38), channel_id=1, source_target_pairs={{2,0},{0,2},{3,1},{1,3},{6,4},{4,6},{7,5},{5,7},{10,8},{8,10},{11,... | collective-permute-start | bytes 196616 | tf_op jit(solution)/shard_map/ppermute | solution.py:315
  24.4 2.2 %collective-permute-done.3.got = bf16[2,128,128]{2,1,0:T(8,128)(2,1)S(1)} collective-permute-done((bf16[2,128,128]{2,1,0:T(8,128)(2,1)S(1)}, bf16[2,128,128]{2,1,0:T(8,128)(2,1)S(1)}, u32[]{:S(2)}, u32[]{:S(2)}) %collective-permute-start.3) | collective-permute-done | bytes 65568 | tf_op jit(solution)/shard_map/ppermute | solution.py:315
  26.6 1.0 %collective-permute-start.5 = (bf16[3,4,2,128,128]{4,3,2,1,0:T(8,128)(2,1)S(1)}, bf16[3,4,2,128,128]{4,3,2,1,0:T(8,128)(2,1)S(1)}, u32[]{:S(2)}, u32[]{:S(2)}) collective-permute-start(bf16[3,4,2,128,128]{4,3,2,1,0:T(8,128)(2,1)S(1)} %get-tuple-element.42.refs_1_), channel_id=1, source_target_pairs={{2,0},{0,2},{3,1},{1,3},{6,4},{4,6},{7,5},{5,7},{10,8},{8,10},{11,... | collective-permute-start | bytes 2359304 | tf_op jit(solution)/shard_map/ppermute | solution.py:315
  27.6 18.6 %all_to_all.10.chunks = bf16[32,8,128]{2,1,0:T(8,128)(2,1)S(1)} all-to-all(bf16[32,8,128]{2,1,0:T(8,128)(2,1)S(1)} %bitcast.14), channel_id=1, replica_groups=mesh['y'=4,'z'=8,'xh'=2,'xl'=2,'c'=2] {'y','z'}, dimensions={0} | all-to-all | bytes 131072 | tf_op jit(solution)/shard_map/all_to_all | solution.py:376
  46.2 0.5 shard_map.82.mine
  46.8 2.7 %shard_map.83.whole = f32[4,2,128,128]{3,2,1,0:T(8,128)S(1)} custom-call(bf16[2,128,128]{2,1,0:T(8,128)(2,1)S(1)} %shard_map.81.phi, bf16[4,4,2,128,128]{4,3,2,1,0:T(8,128)(2,1)} %collective-permute-done.4.whole, bf16[1,4,2,128,128]{4,3,2,1,0:T(8,128)(2,1)S(1)} %copy-done.3, bf16[3,4,2,128,128]{4,3,2,1,0:T(8,128)(2,1)S(1)} %get-tuple-element.42.refs_1_), custom_call_target="tpu_custom_call" | custom-call | flops 1000000000 | bytes 4000000 | tf_op jit(solution)/shard_map/pallas_call | solution.py:302
  49.6 3.4 %collective-permute-start.7 = (bf16[3,4,2,128,128]{4,3,2,1,0:T(8,128)(2,1)S(1)}, bf16[3,4,2,128,128]{4,3,2,1,0:T(8,128)(2,1)S(1)}, u32[]{:S(2)}, u32[]{:S(2)}) collective-permute-start(bf16[3,4,2,128,128]{4,3,2,1,0:T(8,128)(2,1)S(1)} %collective-permute-done.5.refs_1_), channel_id=1, source_target_pairs={{1,0},{0,1},{3,2},{2,3},{5,4},{4,5},{7,6},{6,7},{9,8},{8,9},{11,10... | collective-permute-start | bytes 2359304 | tf_op jit(solution)/shard_map/ppermute | solution.py:315
  53.0 0.1 collective-permute-start.6
  53.1 2.5 %collective-permute-start.8 = (bf16[4,8,128]{2,1,0:T(8,128)(2,1)S(1)}, bf16[4,8,128]{2,1,0:T(8,128)(2,1)S(1)}, u32[]{:S(2)}, u32[]{:S(2)}) collective-permute-start(bf16[4,8,128]{2,1,0:T(8,128)(2,1)S(1)} %shard_map.82.mine), channel_id=1, source_target_pairs={{4,0},{0,4},{5,1},{1,5},{6,2},{2,6},{7,3},{3,7},{12,8},{8,12},{13,... | collective-permute-start | bytes 24584 | tf_op jit(solution)/shard_map/ppermute | solution.py:315
  55.5 0.8 %shard_map.84.whole = f32[4,2,128,128]{3,2,1,0:T(8,128)S(1)} custom-call(bf16[2,128,128]{2,1,0:T(8,128)(2,1)S(1)} %shard_map.81.phi, f32[4,2,128,128]{3,2,1,0:T(8,128)S(1)} %shard_map.83.whole, bf16[1,4,2,128,128]{4,3,2,1,0:T(8,128)(2,1)S(1)} %collective-permute-done.1.refs_0_, bf16[3,4,2,128,128]{4,3,2,1,0:T(8,128)(2,1)S(1)} %collective-permute-done.5.refs_1_), custom_call_target="tpu_custom_call" | custom-call | flops 500000000 | bytes 2000000 | tf_op jit(solution)/shard_map/pallas_call | solution.py:302
  56.4 0.8 %shard_map.85.looped = f32[4,2,128,128]{3,2,1,0:T(8,128)S(1)} custom-call(bf16[2,128,128]{2,1,0:T(8,128)(2,1)S(1)} %shard_map.81.phi, f32[4,2,128,128]{3,2,1,0:T(8,128)S(1)} %shard_map.84.whole, bf16[1,4,2,128,128]{4,3,2,1,0:T(8,128)(2,1)S(1)} %collective-permute-done.6.refs_0_, bf16[3,4,2,128,128]{4,3,2,1,0:T(8,128)(2,1)S(1)} %collective-permute-done.7.refs_1_), custom_call_target="tpu_custom_call" | custom-call | flops 500000000 | bytes 2000000 | tf_op jit(solution)/shard_map/pallas_call | solution.py:302
  57.2 0.6 shard_map.86
  57.8 13.1 %all_to_all.11.spread = bf16[32,4,8,128]{3,2,1,0:T(8,128)(2,1)S(1)} all-to-all(bf16[32,4,8,128]{3,2,1,0:T(8,128)(2,1)S(1)} %shard_map.86), channel_id=1, replica_groups=mesh['y'=4,'z'=8,'xh'=2,'xl'=2,'c'=2] {'y','z'}, dimensions={0} | all-to-all | bytes 524288 | tf_op jit(solution)/shard_map/all_to_all | solution.py:406
  70.9 0.7 shard_map.87
  71.6 0.7 collective-permute-start.10
  72.3 3.9 %collective-permute-start.11 = (f32[72,128]{1,0:T(8,128)S(1)}, f32[72,128]{1,0:T(8,128)S(1)}, u32[]{:S(2)}, u32[]{:S(2)}) collective-permute-start(f32[72,128]{1,0:T(8,128)S(1)} %get-tuple-element.51), channel_id=1, source_target_pairs={{1,0},{2,1},{3,2},{0,3},{5,4},{6,5},{7,6},{4,7},{9,8},{10,9},{11,1... | collective-permute-start | bytes 110600 | tf_op jit(solution)/shard_map/ppermute | solution.py:315
  76.3 0.7 collective-permute-start.9
  77.0 2.6 %collective-permute-done.11.got3 = f32[72,128]{1,0:T(8,128)S(1)} collective-permute-done((f32[72,128]{1,0:T(8,128)S(1)}, f32[72,128]{1,0:T(8,128)S(1)}, u32[]{:S(2)}, u32[]{:S(2)}) %collective-permute-start.11) | collective-permute-done | bytes 36896 | tf_op jit(solution)/shard_map/ppermute | solution.py:315
  79.6 1.2 %shard_map.88 = (bf16[4,2,32,128]{3,2,1,0:T(8,128)(2,1)}, f32[2,2,2,4]{3,2,1,0:T(2,128)}) custom-call(s32[13]{0:T(128)S(1)} %concatenate.3.ints, f32[8,128]{1,0:T(8,128)S(1)} %get-tuple-element.48.pair, bf16[2,128,128]{2,1,0:T(8,128)(2,1)S(1)} %shard_map.81.phi, f32[72,128]{1,0:T(8,128)S(1)} %collective-permute-done.9.got1, ...), custom_call_target="tpu_custom_call" | custom-call | flops 100000 | bytes 1000000 | tf_op jit(solution)/shard_map/pallas_call | solution.py:302
  (23 shorter events, 0.1 us)
Async XLA Ops:
  0.6 5.9 %copy-start.1 = (bf16[1,2,3,4,256,128]{5,4,3,2,1,0:T(8,128)(2,1)S(1)}, bf16[1,2,3,4,256,128]{5,4,3,2,1,0:T(8,128)(2,1)}, u32[]{:S(2)}) copy-start(bf16[1,2,3,4,256,128]{5,4,3,2,1,0:T(8,128)(2,1)} %param.6) | copy-start | bytes 4718596
  0.6 5.6 %copy-start = (bf16[1,4,1,4,2,128,128]{6,5,4,3,2,1,0:T(8,128)(2,1)S(1)}, bf16[1,4,1,4,2,128,128]{6,5,4,3,2,1,0:T(8,128)(2,1)}, u32[]{:S(2)}) copy-start(bf16[1,4,1,4,2,128,128]{6,5,4,3,2,1,0:T(8,128)(2,1)} %param.8) | copy-start | bytes 3145732
  0.7 5.7 %copy-start.5 = (s32[2,3]{1,0:T(2,128)S(1)}, s32[2,3]{1,0:T(2,128)}, u32[]{:S(2)}) copy-start(s32[2,3]{1,0:T(2,128)} %param.9) | copy-start | bytes 76
  0.7 5.7 %copy-start.6 = (s32[2,2]{1,0:T(2,128)S(1)}, s32[2,2]{1,0:T(2,128)}, u32[]{:S(2)}) copy-start(s32[2,2]{1,0:T(2,128)} %param.10) | copy-start | bytes 52
  2.9 15.3 %collective-permute-start = (bf16[2,3,256,128]{3,2,1,0:T(8,128)(2,1)}, bf16[2,3,256,128]{3,2,1,0:T(8,128)(2,1)S(1)}, u32[]{:S(2)}, u32[]{:S(2)}) collective-permute-start(bf16[2,3,256,128]{3,2,1,0:T(8,128)(2,1)} %get-tuple-element.28), channel_id=1, source_target_pairs={{1,0},{2,1},{3,2},{0,3},{5,4},{6,5},{7,6},{4,7},{9,8},{10,9},{11,1... | collective-permute-start | bytes 1179656 | tf_op jit(solution)/shard_map/ppermute | solution.py:315
  6.2 40.6 %collective-permute-start.4 = (bf16[4,4,2,128,128]{4,3,2,1,0:T(8,128)(2,1)S(1)}, bf16[4,4,2,128,128]{4,3,2,1,0:T(8,128)(2,1)}, u32[]{:S(2)}, u32[]{:S(2)}) collective-permute-start(bf16[4,4,2,128,128]{4,3,2,1,0:T(8,128)(2,1)S(1)} %bitcast.12), channel_id=1, source_target_pairs={{1,0},{0,1},{3,2},{2,3},{5,4},{4,5},{7,6},{6,7},{9,8},{8,9},{11,10... | collective-permute-start | bytes 3145736 | tf_op jit(solution)/shard_map/ppermute | solution.py:315
  6.3 11.9 %collective-permute-start.1 = (bf16[1,4,2,128,128]{4,3,2,1,0:T(8,128)(2,1)}, bf16[1,4,2,128,128]{4,3,2,1,0:T(8,128)(2,1)S(1)}, u32[]{:S(2)}, u32[]{:S(2)}) collective-permute-start(bf16[1,4,2,128,128]{4,3,2,1,0:T(8,128)(2,1)} %get-tuple-element.30.refs_0_), channel_id=1, source_target_pairs={{2,0},{0,2},{3,1},{1,3},{6,4},{4,6},{7,5},{5,7},{10,8},{8,10},{11,... | collective-permute-start | bytes 786440 | tf_op jit(solution)/shard_map/ppermute | solution.py:315
  6.6 0.9 %copy-start.4 = (bf16[1,3,3,3,2,4,256]{6,5,4,3,2,1,0:T(4,128)(2,1)S(1)}, bf16[1,3,3,3,2,4,256]{6,5,4,3,2,1,0:T(4,128)(2,1)}, u32[]{:S(2)}) copy-start(bf16[1,3,3,3,2,4,256]{6,5,4,3,2,1,0:T(4,128)(2,1)} %param.7) | copy-start | bytes 331780
  18.2 28.0 %copy-start.2 = (s32[4]{0:T(128)S(1)}, s32[4]{0:T(128)}, u32[]{:S(2)}) copy-start(s32[4]{0:T(128)} %sources.3) | copy-start | bytes 52
  18.3 28.5 %copy-start.3 = (bf16[1,4,2,128,128]{4,3,2,1,0:T(8,128)(2,1)S(1)}, bf16[1,4,2,128,128]{4,3,2,1,0:T(8,128)(2,1)}, u32[]{:S(2)}) copy-start(bf16[1,4,2,128,128]{4,3,2,1,0:T(8,128)(2,1)} %get-tuple-element.30.refs_0_) | copy-start | bytes 786436
  20.4 1.7 %collective-permute-start.2 = (f32[2,2,128,128]{3,2,1,0:T(8,128)S(1)}, f32[2,2,128,128]{3,2,1,0:T(8,128)S(1)}, u32[]{:S(2)}, u32[]{:S(2)}) collective-permute-start(f32[2,2,128,128]{3,2,1,0:T(8,128)S(1)} %get-tuple-element.35), channel_id=1, source_target_pairs={{1,0},{0,1},{3,2},{2,3},{5,4},{4,5},{7,6},{6,7},{9,8},{8,9},{11,10... | collective-permute-start | bytes 786440 | tf_op jit(solution)/shard_map/ppermute | solution.py:315
  22.6 4.0 %collective-permute-start.3 = (bf16[2,128,128]{2,1,0:T(8,128)(2,1)S(1)}, bf16[2,128,128]{2,1,0:T(8,128)(2,1)S(1)}, u32[]{:S(2)}, u32[]{:S(2)}) collective-permute-start(bf16[2,128,128]{2,1,0:T(8,128)(2,1)S(1)} %get-tuple-element.38), channel_id=1, source_target_pairs={{2,0},{0,2},{3,1},{1,3},{6,4},{4,6},{7,5},{5,7},{10,8},{8,10},{11,... | collective-permute-start | bytes 196616 | tf_op jit(solution)/shard_map/ppermute | solution.py:315
  26.6 23.0 %collective-permute-start.5 = (bf16[3,4,2,128,128]{4,3,2,1,0:T(8,128)(2,1)S(1)}, bf16[3,4,2,128,128]{4,3,2,1,0:T(8,128)(2,1)S(1)}, u32[]{:S(2)}, u32[]{:S(2)}) collective-permute-start(bf16[3,4,2,128,128]{4,3,2,1,0:T(8,128)(2,1)S(1)} %get-tuple-element.42.refs_1_), channel_id=1, source_target_pairs={{2,0},{0,2},{3,1},{1,3},{6,4},{4,6},{7,5},{5,7},{10,8},{8,10},{11,... | collective-permute-start | bytes 2359304 | tf_op jit(solution)/shard_map/ppermute | solution.py:315
  49.6 6.8 %collective-permute-start.7 = (bf16[3,4,2,128,128]{4,3,2,1,0:T(8,128)(2,1)S(1)}, bf16[3,4,2,128,128]{4,3,2,1,0:T(8,128)(2,1)S(1)}, u32[]{:S(2)}, u32[]{:S(2)}) collective-permute-start(bf16[3,4,2,128,128]{4,3,2,1,0:T(8,128)(2,1)S(1)} %collective-permute-done.5.refs_1_), channel_id=1, source_target_pairs={{1,0},{0,1},{3,2},{2,3},{5,4},{4,5},{7,6},{6,7},{9,8},{8,9},{11,10... | collective-permute-start | bytes 2359304 | tf_op jit(solution)/shard_map/ppermute | solution.py:315
  53.0 3.4 %collective-permute-start.6 = (bf16[1,4,2,128,128]{4,3,2,1,0:T(8,128)(2,1)S(1)}, bf16[1,4,2,128,128]{4,3,2,1,0:T(8,128)(2,1)S(1)}, u32[]{:S(2)}, u32[]{:S(2)}) collective-permute-start(bf16[1,4,2,128,128]{4,3,2,1,0:T(8,128)(2,1)S(1)} %collective-permute-done.1.refs_0_), channel_id=1, source_target_pairs={{1,0},{0,1},{3,2},{2,3},{5,4},{4,5},{7,6},{6,7},{9,8},{8,9},{11,10... | collective-permute-start | bytes 786440 | tf_op jit(solution)/shard_map/ppermute | solution.py:315
  53.1 4.2 %collective-permute-start.8 = (bf16[4,8,128]{2,1,0:T(8,128)(2,1)S(1)}, bf16[4,8,128]{2,1,0:T(8,128)(2,1)S(1)}, u32[]{:S(2)}, u32[]{:S(2)}) collective-permute-start(bf16[4,8,128]{2,1,0:T(8,128)(2,1)S(1)} %shard_map.82.mine), channel_id=1, source_target_pairs={{4,0},{0,4},{5,1},{1,5},{6,2},{2,6},{7,3},{3,7},{12,8},{8,12},{13,... | collective-permute-start | bytes 24584 | tf_op jit(solution)/shard_map/ppermute | solution.py:315
  71.6 5.4 %collective-permute-start.10 = (f32[72,128]{1,0:T(8,128)S(1)}, f32[72,128]{1,0:T(8,128)S(1)}, u32[]{:S(2)}, u32[]{:S(2)}) collective-permute-start(f32[72,128]{1,0:T(8,128)S(1)} %get-tuple-element.50), channel_id=1, source_target_pairs={{2,0},{3,1},{0,2},{1,3},{6,4},{7,5},{4,6},{5,7},{10,8},{11,9},{8,1... | collective-permute-start | bytes 110600 | tf_op jit(solution)/shard_map/ppermute | solution.py:315
  72.3 7.2 %collective-permute-start.11 = (f32[72,128]{1,0:T(8,128)S(1)}, f32[72,128]{1,0:T(8,128)S(1)}, u32[]{:S(2)}, u32[]{:S(2)}) collective-permute-start(f32[72,128]{1,0:T(8,128)S(1)} %get-tuple-element.51), channel_id=1, source_target_pairs={{1,0},{2,1},{3,2},{0,3},{5,4},{6,5},{7,6},{4,7},{9,8},{10,9},{11,1... | collective-permute-start | bytes 110600 | tf_op jit(solution)/shard_map/ppermute | solution.py:315
  76.3 3.3 %collective-permute-start.9 = (f32[72,128]{1,0:T(8,128)S(1)}, f32[72,128]{1,0:T(8,128)S(1)}, u32[]{:S(2)}, u32[]{:S(2)}) collective-permute-start(f32[72,128]{1,0:T(8,128)S(1)} %get-tuple-element.49), channel_id=1, source_target_pairs={{3,0},{0,1},{1,2},{2,3},{7,4},{4,5},{5,6},{6,7},{11,8},{8,9},{9,10... | collective-permute-start | bytes 110600 | tf_op jit(solution)/shard_map/ppermute | solution.py:315

commit v5 on v4

--- a/solution.py
+++ b/solution.py
@@ -305,7 +305,7 @@
         in_specs=[SMEM if x.ndim == 1 else VMEM for x in inputs],
         out_specs=jax.tree.map(lambda _: VMEM, outs),
         scratch_shapes=scratch,
-        compiler_params=pltpu.CompilerParams(vmem_limit_bytes=40 * 2**20),
+        compiler_params=pltpu.CompilerParams(vmem_limit_bytes=(40 if kernel is local_kernel else 20) * 2**20),
         cost_estimate=pl.CostEstimate(flops=flops, bytes_accessed=moved, transcendentals=0),
     )(*inputs)
 

time: 81 us -> 80.9 us (level)
  no operation moved by 1% of the time
where the time goes in v5:
time: 80.9 us; the launch traced here: 80.7 us
  blocking collectives  31.8 us (39%)
  Pallas kernels  23 us (28%)
  starting transfers between devices  18 us (22%)
  waiting for transfers between devices  5.92 us (7%)
  local copies, waits for them, and re-layouts  1.17 us (1%)
  between operations  0.83 us (1%)
    pallas_call x11, Pallas kernels, call(): pl.pallas_call(kernel, out_shape=outs, in_specs=[SMEM if x.ndim == 1 else...  20.8 us
    all_to_all x1, blocking collectives, on_device(): chunks = lax.all_to_all(phi.reshape(32, 8, 128), YZ, 0, 0, tiled=True)  18.6 us
    ppermute x12, starting transfers between devices, partner(): lax.ppermute(value, axis, [((i + distance) % n, i) for i in range(n)])  18 us
    all_to_all x1, blocking collectives, on_device(): spread = lax.all_to_all(spread, YZ, 0, 0, tiled=True)  13.1 us
    ppermute x12, waiting for transfers between devices, partner(): lax.ppermute(value, axis, [((i + distance) % n, i) for i in range(n)])  5.92 us
    pallas_call x1, Pallas kernels, on_device(): pl.pallas_call(pieces_kernel, out_shape=(shaped(2, 3, 256, 128, dtype=BF)...  2.21 us
  transfers between devices with their start and end apart: 12, of which 3 were waited for; matrix products, arithmetic and copies ran while one was open for 0% of the time, Pallas kernels for 23%

profile of v5, /device:TPU:1, one launch (start us, length us, event | category | flops | bytes accessed | tf_op | source)
XLA Modules:
  0.0 80.7 jit_solution(10317162645604047980)
XLA Ops:
  0.7 2.2 %shard_map.77 = (bf16[2,3,256,128]{3,2,1,0:T(8,128)(2,1)}, bf16[1,4,2,128,128]{4,3,2,1,0:T(8,128)(2,1)}) custom-call(bf16[2,3,4,256,128]{4,3,2,1,0:T(8,128)(2,1)} %bitcast.15, bf16[4,4,2,128,128]{4,3,2,1,0:T(8,128)(2,1)} %bitcast.11), custom_call_target="tpu_custom_call" | custom-call | tf_op jit(solution)/shard_map/pallas_call | solution.py:329
  2.9 3.3 %collective-permute-start = (bf16[2,3,256,128]{3,2,1,0:T(8,128)(2,1)}, bf16[2,3,256,128]{3,2,1,0:T(8,128)(2,1)S(1)}, u32[]{:S(2)}, u32[]{:S(2)}) collective-permute-start(bf16[2,3,256,128]{3,2,1,0:T(8,128)(2,1)} %get-tuple-element.28), channel_id=1, source_target_pairs={{1,0},{2,1},{3,2},{0,3},{5,4},{6,5},{7,6},{4,7},{9,8},{10,9},{11,1... | collective-permute-start | bytes 1179656 | tf_op jit(solution)/shard_map/ppermute | solution.py:315
  6.2 0.1 collective-permute-start.4
  6.3 0.1 reshape.16
  6.4 0.1 reshape.17
  6.5 0.1 concatenate.3.ints
  6.6 0.9 %copy-done.4 = bf16[1,3,3,3,2,4,256]{6,5,4,3,2,1,0:T(4,128)(2,1)S(1)} copy-done((bf16[1,3,3,3,2,4,256]{6,5,4,3,2,1,0:T(4,128)(2,1)S(1)}, bf16[1,3,3,3,2,4,256]{6,5,4,3,2,1,0:T(4,128)(2,1)}, u32[]{:S(2)}) %copy-start.4) | copy-done | bytes 110616
  7.5 10.6 %shard_map.78 = (f32[4,512,256]{2,1,0:T(8,128)S(1)}, bf16[2,512,768]{2,1,0:T(8,128)(2,1)S(1)}, f32[1,54,256]{2,1,0:T(8,128)S(1)}) custom-call(s32[13]{0:T(128)S(1)} %concatenate.3.ints, bf16[2,3,4,256,128]{4,3,2,1,0:T(8,128)(2,1)S(1)} %bitcast.16, bf16[54,4,256]{2,1,0:T(4,128)(2,1)S(1)} %bitcast.17), custom_call_target="tpu_custom_call" | custom-call | flops 4000000000 | bytes 5000000 | tf_op jit(solution)/shard_map/pallas_call | solution.py:302
  18.2 0.0 copy-start.2
  18.2 2.1 %shard_map.79 = (f32[2,2,128,128]{3,2,1,0:T(8,128)S(1)}, f32[2,2,128,128]{3,2,1,0:T(8,128)S(1)}, bf16[3,4,2,128,128]{4,3,2,1,0:T(8,128)(2,1)S(1)}) custom-call(s32[13]{0:T(128)S(1)} %concatenate.3.ints, bf16[2,3,256,128]{3,2,1,0:T(8,128)(2,1)S(1)} %collective-permute-done.halo, f32[1,54,256]{2,1,0:T(8,128)S(1)} %get-tuple-element.29.links, ...), custom_call_target="tpu_custom_call" | custom-call | flops 500000000 | bytes 5000000 | tf_op jit(solution)/shard_map/pallas_call | solution.py:302
  20.2 0.5 collective-permute-start.2
  20.7 1.2 %collective-permute-done.2.got = f32[2,2,128,128]{3,2,1,0:T(8,128)S(1)} collective-permute-done((f32[2,2,128,128]{3,2,1,0:T(8,128)S(1)}, f32[2,2,128,128]{3,2,1,0:T(8,128)S(1)}, u32[]{:S(2)}, u32[]{:S(2)}) %collective-permute-start.2) | collective-permute-done | bytes 262176 | tf_op jit(solution)/shard_map/ppermute | solution.py:315
  21.9 0.6 shard_map.80
  22.5 1.8 %collective-permute-start.3 = (bf16[2,128,128]{2,1,0:T(8,128)(2,1)S(1)}, bf16[2,128,128]{2,1,0:T(8,128)(2,1)S(1)}, u32[]{:S(2)}, u32[]{:S(2)}) collective-permute-start(bf16[2,128,128]{2,1,0:T(8,128)(2,1)S(1)} %get-tuple-element.38), channel_id=1, source_target_pairs={{2,0},{0,2},{3,1},{1,3},{6,4},{4,6},{7,5},{5,7},{10,8},{8,10},{11,... | collective-permute-start | bytes 196616 | tf_op jit(solution)/shard_map/ppermute | solution.py:315
  24.3 2.2 %collective-permute-done.3.got = bf16[2,128,128]{2,1,0:T(8,128)(2,1)S(1)} collective-permute-done((bf16[2,128,128]{2,1,0:T(8,128)(2,1)S(1)}, bf16[2,128,128]{2,1,0:T(8,128)(2,1)S(1)}, u32[]{:S(2)}, u32[]{:S(2)}) %collective-permute-start.3) | collective-permute-done | bytes 65568 | tf_op jit(solution)/shard_map/ppermute | solution.py:315
  26.5 1.0 %collective-permute-start.5 = (bf16[3,4,2,128,128]{4,3,2,1,0:T(8,128)(2,1)S(1)}, bf16[3,4,2,128,128]{4,3,2,1,0:T(8,128)(2,1)S(1)}, u32[]{:S(2)}, u32[]{:S(2)}) collective-permute-start(bf16[3,4,2,128,128]{4,3,2,1,0:T(8,128)(2,1)S(1)} %get-tuple-element.42.refs_1_), channel_id=1, source_target_pairs={{2,0},{0,2},{3,1},{1,3},{6,4},{4,6},{7,5},{5,7},{10,8},{8,10},{11,... | collective-permute-start | bytes 2359304 | tf_op jit(solution)/shard_map/ppermute | solution.py:315
  27.4 18.6 %all_to_all.10.chunks = bf16[32,8,128]{2,1,0:T(8,128)(2,1)S(1)} all-to-all(bf16[32,8,128]{2,1,0:T(8,128)(2,1)S(1)} %bitcast.14), channel_id=1, replica_groups=mesh['y'=4,'z'=8,'xh'=2,'xl'=2,'c'=2] {'y','z'}, dimensions={0} | all-to-all | bytes 131072 | tf_op jit(solution)/shard_map/all_to_all | solution.py:376
  46.1 0.5 shard_map.82.mine
  46.7 2.7 %shard_map.83.whole = f32[4,2,128,128]{3,2,1,0:T(8,128)S(1)} custom-call(bf16[2,128,128]{2,1,0:T(8,128)(2,1)S(1)} %shard_map.81.phi, bf16[4,4,2,128,128]{4,3,2,1,0:T(8,128)(2,1)} %collective-permute-done.4.whole, bf16[1,4,2,128,128]{4,3,2,1,0:T(8,128)(2,1)S(1)} %copy-done.3, bf16[3,4,2,128,128]{4,3,2,1,0:T(8,128)(2,1)S(1)} %get-tuple-element.42.refs_1_), custom_call_target="tpu_custom_call" | custom-call | flops 1000000000 | bytes 4000000 | tf_op jit(solution)/shard_map/pallas_call | solution.py:302
  49.4 3.4 %collective-permute-start.7 = (bf16[3,4,2,128,128]{4,3,2,1,0:T(8,128)(2,1)S(1)}, bf16[3,4,2,128,128]{4,3,2,1,0:T(8,128)(2,1)S(1)}, u32[]{:S(2)}, u32[]{:S(2)}) collective-permute-start(bf16[3,4,2,128,128]{4,3,2,1,0:T(8,128)(2,1)S(1)} %collective-permute-done.5.refs_1_), channel_id=1, source_target_pairs={{1,0},{0,1},{3,2},{2,3},{5,4},{4,5},{7,6},{6,7},{9,8},{8,9},{11,10... | collective-permute-start | bytes 2359304 | tf_op jit(solution)/shard_map/ppermute | solution.py:315
  52.8 0.1 collective-permute-start.6
  52.9 2.5 %collective-permute-start.8 = (bf16[4,8,128]{2,1,0:T(8,128)(2,1)S(1)}, bf16[4,8,128]{2,1,0:T(8,128)(2,1)S(1)}, u32[]{:S(2)}, u32[]{:S(2)}) collective-permute-start(bf16[4,8,128]{2,1,0:T(8,128)(2,1)S(1)} %shard_map.82.mine), channel_id=1, source_target_pairs={{4,0},{0,4},{5,1},{1,5},{6,2},{2,6},{7,3},{3,7},{12,8},{8,12},{13,... | collective-permute-start | bytes 24584 | tf_op jit(solution)/shard_map/ppermute | solution.py:315
  55.4 0.8 %shard_map.84.whole = f32[4,2,128,128]{3,2,1,0:T(8,128)S(1)} custom-call(bf16[2,128,128]{2,1,0:T(8,128)(2,1)S(1)} %shard_map.81.phi, f32[4,2,128,128]{3,2,1,0:T(8,128)S(1)} %shard_map.83.whole, bf16[1,4,2,128,128]{4,3,2,1,0:T(8,128)(2,1)S(1)} %collective-permute-done.1.refs_0_, bf16[3,4,2,128,128]{4,3,2,1,0:T(8,128)(2,1)S(1)} %collective-permute-done.5.refs_1_), custom_call_target="tpu_custom_call" | custom-call | flops 500000000 | bytes 2000000 | tf_op jit(solution)/shard_map/pallas_call | solution.py:302
  56.3 0.8 %shard_map.85.looped = f32[4,2,128,128]{3,2,1,0:T(8,128)S(1)} custom-call(bf16[2,128,128]{2,1,0:T(8,128)(2,1)S(1)} %shard_map.81.phi, f32[4,2,128,128]{3,2,1,0:T(8,128)S(1)} %shard_map.84.whole, bf16[1,4,2,128,128]{4,3,2,1,0:T(8,128)(2,1)S(1)} %collective-permute-done.6.refs_0_, bf16[3,4,2,128,128]{4,3,2,1,0:T(8,128)(2,1)S(1)} %collective-permute-done.7.refs_1_), custom_call_target="tpu_custom_call" | custom-call | flops 500000000 | bytes 2000000 | tf_op jit(solution)/shard_map/pallas_call | solution.py:302
  57.1 0.6 shard_map.86
  57.7 13.1 %all_to_all.11.spread = bf16[32,4,8,128]{3,2,1,0:T(8,128)(2,1)S(1)} all-to-all(bf16[32,4,8,128]{3,2,1,0:T(8,128)(2,1)S(1)} %shard_map.86), channel_id=1, replica_groups=mesh['y'=4,'z'=8,'xh'=2,'xl'=2,'c'=2] {'y','z'}, dimensions={0} | all-to-all | bytes 524288 | tf_op jit(solution)/shard_map/all_to_all | solution.py:406
  70.8 0.7 shard_map.87
  71.5 0.7 collective-permute-start.10
  72.2 3.9 %collective-permute-start.11 = (f32[72,128]{1,0:T(8,128)S(1)}, f32[72,128]{1,0:T(8,128)S(1)}, u32[]{:S(2)}, u32[]{:S(2)}) collective-permute-start(f32[72,128]{1,0:T(8,128)S(1)} %get-tuple-element.51), channel_id=1, source_target_pairs={{1,0},{2,1},{3,2},{0,3},{5,4},{6,5},{7,6},{4,7},{9,8},{10,9},{11,1... | collective-permute-start | bytes 110600 | tf_op jit(solution)/shard_map/ppermute | solution.py:315
  76.1 0.7 collective-permute-start.9
  76.9 2.6 %collective-permute-done.11.got3 = f32[72,128]{1,0:T(8,128)S(1)} collective-permute-done((f32[72,128]{1,0:T(8,128)S(1)}, f32[72,128]{1,0:T(8,128)S(1)}, u32[]{:S(2)}, u32[]{:S(2)}) %collective-permute-start.11) | collective-permute-done | bytes 36896 | tf_op jit(solution)/shard_map/ppermute | solution.py:315
  79.4 1.2 %shard_map.88 = (bf16[4,2,32,128]{3,2,1,0:T(8,128)(2,1)}, f32[2,2,2,4]{3,2,1,0:T(2,128)}) custom-call(s32[13]{0:T(128)S(1)} %concatenate.3.ints, f32[8,128]{1,0:T(8,128)S(1)} %get-tuple-element.48.pair, bf16[2,128,128]{2,1,0:T(8,128)(2,1)S(1)} %shard_map.81.phi, f32[72,128]{1,0:T(8,128)S(1)} %collective-permute-done.9.got1, ...), custom_call_target="tpu_custom_call" | custom-call | flops 100000 | bytes 1000000 | tf_op jit(solution)/shard_map/pallas_call | solution.py:302
  (23 shorter events, 0.1 us)
Async XLA Ops:
  0.6 5.9 %copy-start.1 = (bf16[1,2,3,4,256,128]{5,4,3,2,1,0:T(8,128)(2,1)S(1)}, bf16[1,2,3,4,256,128]{5,4,3,2,1,0:T(8,128)(2,1)}, u32[]{:S(2)}) copy-start(bf16[1,2,3,4,256,128]{5,4,3,2,1,0:T(8,128)(2,1)} %param.6) | copy-start | bytes 4718596
  0.6 5.6 %copy-start = (bf16[1,4,1,4,2,128,128]{6,5,4,3,2,1,0:T(8,128)(2,1)S(1)}, bf16[1,4,1,4,2,128,128]{6,5,4,3,2,1,0:T(8,128)(2,1)}, u32[]{:S(2)}) copy-start(bf16[1,4,1,4,2,128,128]{6,5,4,3,2,1,0:T(8,128)(2,1)} %param.8) | copy-start | bytes 3145732
  0.7 5.7 %copy-start.5 = (s32[2,3]{1,0:T(2,128)S(1)}, s32[2,3]{1,0:T(2,128)}, u32[]{:S(2)}) copy-start(s32[2,3]{1,0:T(2,128)} %param.9) | copy-start | bytes 76
  0.7 5.7 %copy-start.6 = (s32[2,2]{1,0:T(2,128)S(1)}, s32[2,2]{1,0:T(2,128)}, u32[]{:S(2)}) copy-start(s32[2,2]{1,0:T(2,128)} %param.10) | copy-start | bytes 52
  2.9 15.3 %collective-permute-start = (bf16[2,3,256,128]{3,2,1,0:T(8,128)(2,1)}, bf16[2,3,256,128]{3,2,1,0:T(8,128)(2,1)S(1)}, u32[]{:S(2)}, u32[]{:S(2)}) collective-permute-start(bf16[2,3,256,128]{3,2,1,0:T(8,128)(2,1)} %get-tuple-element.28), channel_id=1, source_target_pairs={{1,0},{2,1},{3,2},{0,3},{5,4},{6,5},{7,6},{4,7},{9,8},{10,9},{11,1... | collective-permute-start | bytes 1179656 | tf_op jit(solution)/shard_map/ppermute | solution.py:315
  6.2 40.4 %collective-permute-start.4 = (bf16[4,4,2,128,128]{4,3,2,1,0:T(8,128)(2,1)S(1)}, bf16[4,4,2,128,128]{4,3,2,1,0:T(8,128)(2,1)}, u32[]{:S(2)}, u32[]{:S(2)}) collective-permute-start(bf16[4,4,2,128,128]{4,3,2,1,0:T(8,128)(2,1)S(1)} %bitcast.12), channel_id=1, source_target_pairs={{1,0},{0,1},{3,2},{2,3},{5,4},{4,5},{7,6},{6,7},{9,8},{8,9},{11,10... | collective-permute-start | bytes 3145736 | tf_op jit(solution)/shard_map/ppermute | solution.py:315
  6.3 11.8 %collective-permute-start.1 = (bf16[1,4,2,128,128]{4,3,2,1,0:T(8,128)(2,1)}, bf16[1,4,2,128,128]{4,3,2,1,0:T(8,128)(2,1)S(1)}, u32[]{:S(2)}, u32[]{:S(2)}) collective-permute-start(bf16[1,4,2,128,128]{4,3,2,1,0:T(8,128)(2,1)} %get-tuple-element.30.refs_0_), channel_id=1, source_target_pairs={{2,0},{0,2},{3,1},{1,3},{6,4},{4,6},{7,5},{5,7},{10,8},{8,10},{11,... | collective-permute-start | bytes 786440 | tf_op jit(solution)/shard_map/ppermute | solution.py:315
  6.6 0.9 %copy-start.4 = (bf16[1,3,3,3,2,4,256]{6,5,4,3,2,1,0:T(4,128)(2,1)S(1)}, bf16[1,3,3,3,2,4,256]{6,5,4,3,2,1,0:T(4,128)(2,1)}, u32[]{:S(2)}) copy-start(bf16[1,3,3,3,2,4,256]{6,5,4,3,2,1,0:T(4,128)(2,1)} %param.7) | copy-start | bytes 331780
  18.2 27.9 %copy-start.2 = (s32[4]{0:T(128)S(1)}, s32[4]{0:T(128)}, u32[]{:S(2)}) copy-start(s32[4]{0:T(128)} %sources.3) | copy-start | bytes 52
  18.2 28.5 %copy-start.3 = (bf16[1,4,2,128,128]{4,3,2,1,0:T(8,128)(2,1)S(1)}, bf16[1,4,2,128,128]{4,3,2,1,0:T(8,128)(2,1)}, u32[]{:S(2)}) copy-start(bf16[1,4,2,128,128]{4,3,2,1,0:T(8,128)(2,1)} %get-tuple-element.30.refs_0_) | copy-start | bytes 786436
  20.2 1.7 %collective-permute-start.2 = (f32[2,2,128,128]{3,2,1,0:T(8,128)S(1)}, f32[2,2,128,128]{3,2,1,0:T(8,128)S(1)}, u32[]{:S(2)}, u32[]{:S(2)}) collective-permute-start(f32[2,2,128,128]{3,2,1,0:T(8,128)S(1)} %get-tuple-element.35), channel_id=1, source_target_pairs={{1,0},{0,1},{3,2},{2,3},{5,4},{4,5},{7,6},{6,7},{9,8},{8,9},{11,10... | collective-permute-start | bytes 786440 | tf_op jit(solution)/shard_map/ppermute | solution.py:315
  22.5 4.0 %collective-permute-start.3 = (bf16[2,128,128]{2,1,0:T(8,128)(2,1)S(1)}, bf16[2,128,128]{2,1,0:T(8,128)(2,1)S(1)}, u32[]{:S(2)}, u32[]{:S(2)}) collective-permute-start(bf16[2,128,128]{2,1,0:T(8,128)(2,1)S(1)} %get-tuple-element.38), channel_id=1, source_target_pairs={{2,0},{0,2},{3,1},{1,3},{6,4},{4,6},{7,5},{5,7},{10,8},{8,10},{11,... | collective-permute-start | bytes 196616 | tf_op jit(solution)/shard_map/ppermute | solution.py:315
  26.5 23.0 %collective-permute-start.5 = (bf16[3,4,2,128,128]{4,3,2,1,0:T(8,128)(2,1)S(1)}, bf16[3,4,2,128,128]{4,3,2,1,0:T(8,128)(2,1)S(1)}, u32[]{:S(2)}, u32[]{:S(2)}) collective-permute-start(bf16[3,4,2,128,128]{4,3,2,1,0:T(8,128)(2,1)S(1)} %get-tuple-element.42.refs_1_), channel_id=1, source_target_pairs={{2,0},{0,2},{3,1},{1,3},{6,4},{4,6},{7,5},{5,7},{10,8},{8,10},{11,... | collective-permute-start | bytes 2359304 | tf_op jit(solution)/shard_map/ppermute | solution.py:315
  49.4 6.8 %collective-permute-start.7 = (bf16[3,4,2,128,128]{4,3,2,1,0:T(8,128)(2,1)S(1)}, bf16[3,4,2,128,128]{4,3,2,1,0:T(8,128)(2,1)S(1)}, u32[]{:S(2)}, u32[]{:S(2)}) collective-permute-start(bf16[3,4,2,128,128]{4,3,2,1,0:T(8,128)(2,1)S(1)} %collective-permute-done.5.refs_1_), channel_id=1, source_target_pairs={{1,0},{0,1},{3,2},{2,3},{5,4},{4,5},{7,6},{6,7},{9,8},{8,9},{11,10... | collective-permute-start | bytes 2359304 | tf_op jit(solution)/shard_map/ppermute | solution.py:315
  52.8 3.4 %collective-permute-start.6 = (bf16[1,4,2,128,128]{4,3,2,1,0:T(8,128)(2,1)S(1)}, bf16[1,4,2,128,128]{4,3,2,1,0:T(8,128)(2,1)S(1)}, u32[]{:S(2)}, u32[]{:S(2)}) collective-permute-start(bf16[1,4,2,128,128]{4,3,2,1,0:T(8,128)(2,1)S(1)} %collective-permute-done.1.refs_0_), channel_id=1, source_target_pairs={{1,0},{0,1},{3,2},{2,3},{5,4},{4,5},{7,6},{6,7},{9,8},{8,9},{11,10... | collective-permute-start | bytes 786440 | tf_op jit(solution)/shard_map/ppermute | solution.py:315
  52.9 4.2 %collective-permute-start.8 = (bf16[4,8,128]{2,1,0:T(8,128)(2,1)S(1)}, bf16[4,8,128]{2,1,0:T(8,128)(2,1)S(1)}, u32[]{:S(2)}, u32[]{:S(2)}) collective-permute-start(bf16[4,8,128]{2,1,0:T(8,128)(2,1)S(1)} %shard_map.82.mine), channel_id=1, source_target_pairs={{4,0},{0,4},{5,1},{1,5},{6,2},{2,6},{7,3},{3,7},{12,8},{8,12},{13,... | collective-permute-start | bytes 24584 | tf_op jit(solution)/shard_map/ppermute | solution.py:315
  71.5 5.4 %collective-permute-start.10 = (f32[72,128]{1,0:T(8,128)S(1)}, f32[72,128]{1,0:T(8,128)S(1)}, u32[]{:S(2)}, u32[]{:S(2)}) collective-permute-start(f32[72,128]{1,0:T(8,128)S(1)} %get-tuple-element.50), channel_id=1, source_target_pairs={{2,0},{3,1},{0,2},{1,3},{6,4},{7,5},{4,6},{5,7},{10,8},{11,9},{8,1... | collective-permute-start | bytes 110600 | tf_op jit(solution)/shard_map/ppermute | solution.py:315
  72.2 7.2 %collective-permute-start.11 = (f32[72,128]{1,0:T(8,128)S(1)}, f32[72,128]{1,0:T(8,128)S(1)}, u32[]{:S(2)}, u32[]{:S(2)}) collective-permute-start(f32[72,128]{1,0:T(8,128)S(1)} %get-tuple-element.51), channel_id=1, source_target_pairs={{1,0},{2,1},{3,2},{0,3},{5,4},{6,5},{7,6},{4,7},{9,8},{10,9},{11,1... | collective-permute-start | bytes 110600 | tf_op jit(solution)/shard_map/ppermute | solution.py:315
  76.1 3.3 %collective-permute-start.9 = (f32[72,128]{1,0:T(8,128)S(1)}, f32[72,128]{1,0:T(8,128)S(1)}, u32[]{:S(2)}, u32[]{:S(2)}) collective-permute-start(f32[72,128]{1,0:T(8,128)S(1)} %get-tuple-element.49), channel_id=1, source_target_pairs={{3,0},{0,1},{1,2},{2,3},{7,4},{4,5},{5,6},{6,7},{11,8},{8,9},{9,10... | collective-permute-start | bytes 110600 | tf_op jit(solution)/shard_map/ppermute | solution.py:315
